TPU v7x, 128 devices: a whole 4x4x4 slice. The times are simulated.
128 devices in a mesh: sec: 2 (over core), tile: 64 (over x, y, z).
Axes of the slice: x: 4, y: 4, z: 4, core: 2. Of those that a mesh axis runs over, the one named last changes fastest.
Arguments:
- atm_state: float32 [2, 32768, 4, 128], P('sec', 'tile'), may hold values from -8 to 8, as said below
- routes: int32 [2, 32768, 1], P('sec', 'tile'), may hold values from 0 to 63; in each aligned block of 512 rows (0 to 511, 512 to 1023, ..., all dimensions but the last counted through in order) at most 16 rows name the same one
- dst_block: int32 [2, 32768], P('sec', 'tile'), may hold values from 0 to 127
- weight_index: int32 [2, 32768], P('sec', 'tile'), may hold values from 0 to 15
- area_table: float32 [16, 128], replicated, may hold values from 0.1 to 1
- ocean_temp: float32 [2, 80, 1024, 1024], P('sec', None, 'tile'), may hold values from -6 to 6
- vel_u: float32 [2, 80, 1024, 1024], P('sec', None, 'tile'), may hold values from -0.6 to 0.6
- vel_v: float32 [2, 80, 1024, 1024], P('sec', None, 'tile'), may hold values from -0.6 to 0.6
- depth_levels: int32 [2, 1024, 1024], P('sec', 'tile'), may hold values from 0 to 80, as said below
Outputs:
- following_water_warmth: float32 [2, 80, 1024, 1024], P('sec', None, 'tile')
- coupler_skin_warmth: float32 [2, 32768, 128], P('sec', 'tile')
Inputs may be any that keep to these rules, and one draw needn't show every extreme that they name: `routes`: among the 512 exchange blocks of one atmosphere device at most 16 map to one ocean tile, and exactly 16 do for some pair in every draw. `atm_state`: channel 0 (wind speed) lies in 0.5 to 4. `depth_levels`: about a quarter of the columns are land.
All inputs are finite; a program needn't handle non-finite values.
Results may differ from a plain program's by a relative error of at most 0.000071.
Values sent between devices are 32-bit elements; how exact they have to be, the bound alone decides.
No kernel may reach another device: no remote copies, remote signals or barrier semaphores. Data moves between devices by JAX's collectives and lax.ppermute only.
A program may use at most 256 MiB of HBM per device.

v0:
```python
import jax
import jax.numpy as jnp
from jax import lax
from jax.sharding import PartitionSpec as P

heat_diffusion = 0.12
vertical_mixing = 0.2
flux_gain = 0.5


def passed_along(value, axis, steps):
    count = lax.axis_size(axis)
    initial, last = (max(0, -steps), min(count, count - steps))
    return lax.ppermute(value, axis, [(source, source + steps) for source in range(initial, last)])


def extended(array, sides, width):
    for axis, dim in sides:
        size, length = (lax.axis_size(axis), array.shape[dim])
        up = [(i, (i + 1) % size) for i in range(size - 1)]
        down = [(j, i) for i, j in up]
        last = lax.slice_in_dim(array, length - width, length, axis=dim)
        initial = lax.slice_in_dim(array, 0, width, axis=dim)
        before = lax.ppermute(last, axis, up)
        after = lax.ppermute(initial, axis, down)
        array = jnp.concatenate([before, array, after], axis=dim)
    return array


def bulk_flux(state, surface_temp):
    speed = state[..., 0, :]
    air = state[..., 1, :]
    humidity = state[..., 2, :]
    radiation = state[..., 3, :]
    contrast = surface_temp - air
    transfer = 0.8 + 0.4 * jnp.tanh(contrast)
    saturation = 0.6 * jnp.exp(0.3 * surface_temp)
    return radiation - transfer * speed * (contrast + 1.5 * (saturation - humidity))


def march_forward(padded_field, driving_heat_input):
    field = padded_field[0]
    zonal = padded_field[1]
    meridional = padded_field[2]
    wetness = padded_field[3]
    centre = field[:, 1:-1]
    wet_c = wetness[:, 1:-1]
    zonal_c = zonal[:, 1:-1]
    merid_c = meridional[:, 1:-1]
    east = jnp.roll(centre, -1, axis=2)
    west = jnp.roll(centre, 1, axis=2)
    wet_e = jnp.roll(wet_c, -1, axis=2)
    wet_w = jnp.roll(wet_c, 1, axis=2)
    north = field[:, 2:]
    south = field[:, :-2]
    wet_n = wetness[:, 2:]
    wet_s = wetness[:, :-2]
    flux_east = 0.25 * (zonal_c + jnp.roll(zonal_c, -1, axis=2)) * (centre + east) * wet_c * wet_e
    flux_west = jnp.roll(flux_east, 1, axis=2)
    flux_north = 0.25 * (merid_c + meridional[:, 2:]) * (centre + north) * wet_c * wet_n
    flux_south = 0.25 * (meridional[:, :-2] + merid_c) * (south + centre) * wet_s * wet_c
    spread = heat_diffusion * (
        wet_e * (east - centre)
        + wet_w * (west - centre)
        + wet_n * (north - centre)
        + wet_s * (south - centre)
    )
    above = jnp.pad(centre[:-1], ((1, 0), (0, 0), (0, 0)))
    below = jnp.pad(centre[1:], ((0, 1), (0, 0), (0, 0)))
    wet_above = jnp.pad(wet_c[:-1], ((1, 0), (0, 0), (0, 0)))
    wet_below = jnp.pad(wet_c[1:], ((0, 1), (0, 0), (0, 0)))
    mixing = vertical_mixing * (wet_above * (above - centre) + wet_below * (below - centre))
    tendency = spread + mixing - (flux_east - flux_west) - (flux_north - flux_south)
    surface = jnp.concatenate(
        [(flux_gain * driving_heat_input)[None], jnp.zeros_like(centre[1:])], axis=0
    )
    return centre + wet_c * (tendency + surface)


def body(
    atm_state, routes, dst_block, weight_index, area_table, ocean_temp, vel_u, vel_v, depth_levels
):
    tiles = lax.axis_size("tile")
    block_count = atm_state.shape[1]
    patch_breadth = atm_state.shape[3]
    capacity = max(2, 2 * block_count // tiles)
    slot_count = tiles * capacity
    marine_indicator = lax.axis_index("sec") == 1
    dest_tile = routes[0, :, 0]
    block_id = dst_block[0]
    table_row = weight_index[0]
    owner_hits = (dest_tile[:, None] == jnp.arange(tiles, dtype=jnp.int32)[None, :]).astype(
        jnp.int32
    )
    earlier = jnp.cumsum(owner_hits, axis=0) - owner_hits
    position = jnp.sum(earlier * owner_hits, axis=1)
    patch_position_number = dest_tile * capacity + position
    entries = (
        jnp.full((slot_count, 2), -1, jnp.int32)
        .at[patch_position_number]
        .set(jnp.stack([block_id, table_row], axis=1))
    )
    temp_local = ocean_temp[0]
    levels_z, rows_local, cells_x = temp_local.shape
    marine_patches = rows_local * cells_x // patch_breadth
    top_blocks = temp_local[0].reshape(marine_patches, patch_breadth)
    packed = (
        jnp.zeros((slot_count,) + atm_state.shape[2:], jnp.float32)
        .at[patch_position_number]
        .set(atm_state[0])
    )
    moved_state, moved_entries = (
        lax.all_to_all(packed, "tile", split_axis=0, concat_axis=0, tiled=True),
        lax.all_to_all(entries, "tile", split_axis=0, concat_axis=0, tiled=True),
    )
    moved_state, moved_entries = passed_along((moved_state, moved_entries), "sec", 1)
    recv_block = moved_entries[:, 0]
    is_live = (recv_block >= 0).astype(jnp.float32)
    safe_block = jnp.maximum(recv_block, 0)
    safe_row = jnp.maximum(moved_entries[:, 1], 0)
    heat = bulk_flux(moved_state, top_blocks[safe_block])
    weights = area_table[safe_row] * is_live[:, None]
    weighted = weights * heat
    selector = (jnp.arange(marine_patches, dtype=jnp.int32)[:, None] == recv_block[None, :]).astype(
        jnp.float32
    )
    heat_sum = jnp.dot(
        selector, weighted, precision=lax.Precision.HIGHEST, preferred_element_type=jnp.float32
    )
    area_sum = jnp.dot(
        selector, weights, precision=lax.Precision.HIGHEST, preferred_element_type=jnp.float32
    )
    driving_heat_input = (heat_sum / jnp.maximum(area_sum, 1.0)).reshape(rows_local, cells_x)
    level_ids = jnp.arange(levels_z, dtype=jnp.int32)
    wetness = (level_ids[:, None, None] < depth_levels[0][None]).astype(jnp.float32)
    stacked = jnp.stack([temp_local, vel_u[0], vel_v[0], wetness])
    padded_field = extended(stacked, (("tile", 2),), 1)
    revised_warmth = lax.cond(
        marine_indicator,
        march_forward,
        lambda grid, push: jnp.zeros_like(temp_local),
        padded_field,
        driving_heat_input,
    )
    fresh_uppermost_layer = revised_warmth[0].reshape(marine_patches, patch_breadth)
    received_patches = fresh_uppermost_layer[safe_block]
    received_patches = passed_along(received_patches, "sec", -1)
    received_patches = lax.all_to_all(
        received_patches, "tile", split_axis=0, concat_axis=0, tiled=True
    )
    tile_skin_warmth = received_patches[patch_position_number]
    following_water_warmth = jnp.where(marine_indicator, revised_warmth, 0.0)[None]
    coupler_skin_warmth = jnp.where(marine_indicator, 0.0, tile_skin_warmth)[None]
    return (following_water_warmth, coupler_skin_warmth)


def solution(mesh):
    return jax.shard_map(
        body,
        mesh=mesh,
        in_specs=(
            P("sec", "tile", None, None),
            P("sec", "tile", None),
            P("sec", "tile"),
            P("sec", "tile"),
            P(),
            P("sec", None, "tile", None),
            P("sec", None, "tile", None),
            P("sec", None, "tile", None),
            P("sec", "tile", None),
        ),
        out_specs=(P("sec", None, "tile", None), P("sec", "tile", None)),
        check_vma=False,
    )
```

profile of v0, /device:TPU:0, one launch (start us, length us, event | category | flops | bytes accessed | tf_op | source)
XLA Modules:
  0.0 330.0 jit_solution(6744469382774034055)
XLA Ops:
  0.6 0.0 copy-start
  0.6 0.7 fusion.59
  1.3 1.2 reduce-window.6
  2.6 0.2 slice_reduce_fusion
  2.8 0.8 fusion.58
  3.6 0.7 compare_select_fusion
  4.3 0.7 pad_add_fusion
  5.0 0.1 copy.19
  5.2 0.0 copy-start.7
  5.2 1.8 scatter_custom_fusion
  7.0 1.1 copy.21
  8.1 11.5 %all-to-all-start = ((s32[64,16,2]{1,2,0:T(2,128)}), s32[64,16,2]{1,2,0:T(2,128)S(1)}, u32[]{:S(2)}, u32[]{:S(2)}) async-start(s32[64,16,2]{1,2,0:T(2,128)} %copy.21), calls=%async_computation | async-start | bytes 131072 | tf_op jit(solution)/shard_map/all_to_all | solution.py:114
  19.6 1.6 broadcast_in_dim.16
  21.2 50.3 %scatter_fusion = f32[1024,4,128]{2,1,0:T(4,128)} fusion(f32[1024,4,128]{2,1,0:T(4,128)} %broadcast_in_dim.16, s32[512]{0:T(512)S(1)} %bitcast.97, f32[512,4,128]{2,1,0:T(4,128)} %bitcast.92), kind=kCustom, calls=%fused_computation.5 | custom fusion | bytes 3147776 | tf_op jit(solution)/shard_map/scatter | solution.py:110
  71.5 0.0 all-to-all-done
  71.5 10.3 %all-to-all-start.1 = ((f32[1024,4,128]{2,1,0:T(4,128)}), f32[1024,4,128]{2,1,0:T(4,128)S(1)}, u32[]{:S(2)}, u32[]{:S(2)}) async-start(f32[1024,4,128]{2,1,0:T(4,128)} %scatter_fusion), calls=%async_computation.1 | async-start | bytes 4194304 | tf_op jit(solution)/shard_map/all_to_all | solution.py:113
  81.9 0.7 fusion.23
  82.5 0.0 copy-start.3
  82.5 0.0 slice-start
  82.6 10.0 %pad_maximum_fusion.6 = (f32[4,80,1,1024]{3,2,1,0:T(1,128)}, f32[4,80,1,1024]{3,2,1,0:T(1,128)}) fusion(f32[1,80,16,1024]{3,2,1,0:T(8,128)S(1)} %fusion.23, f32[1,80,16,1024]{3,2,1,0:T(8,128)} %param.18, f32[1,80,16,1024]{3,2,1,0:T(8,128)} %param.17, f32[1,80,16,1024]{3,2,1,0:T(8,128)} %param.16), kind=kLoop, calls=%fused_computation.49 | loop fusion | flops 1966080 | bytes 23592960 | tf_op jit(solution)/shard_map/slice | solution.py:22
  92.6 4.6 %collective-permute-start = (f32[4,80,1,1024]{3,2,1,0:T(1,128)}, f32[4,80,1,1024]{3,2,1,0:T(1,128)}, u32[]{:S(2)}, u32[]{:S(2)}) collective-permute-start(f32[4,80,1,1024]{3,2,1,0:T(1,128)} %get-tuple-element.47), channel_id=1, source_target_pairs={{0,1},{1,2},{2,3},{3,4},{4,5},{5,6},{6,7},{7,8},{8,9},{9,10},{10,1... | collective-permute-start | bytes 3932168 | tf_op jit(solution)/shard_map/ppermute | solution.py:24
  97.2 1.3 collective-permute-start.1
  98.5 0.1 all_to_all.21
  98.6 1.3 collective-permute-start.2
  99.9 0.8 collective-permute-done.2
  100.7 2.8 gather_fusion
  103.6 1.2 fusion.42
  104.7 6.2 %all-to-all-done.1 = f32[1024,4,128]{2,1,0:T(4,128)S(1)} async-done(((f32[1024,4,128]{2,1,0:T(4,128)}), f32[1024,4,128]{2,1,0:T(4,128)S(1)}, u32[]{:S(2)}, u32[]{:S(2)}) %all-to-all-start.1) | async-done | bytes 2097184 | tf_op jit(solution)/shard_map/all_to_all | solution.py:113
  111.0 1.5 copy.23
  112.4 2.6 collective-permute-start.3
  115.1 2.8 gather_fusion.1
  117.9 15.2 %collective-permute-done = f32[4,80,1,1024]{3,2,1,0:T(1,128)} collective-permute-done((f32[4,80,1,1024]{3,2,1,0:T(1,128)}, f32[4,80,1,1024]{3,2,1,0:T(1,128)}, u32[]{:S(2)}, u32[]{:S(2)}) %collective-permute-start) | collective-permute-done | bytes 1310752 | tf_op jit(solution)/shard_map/ppermute | solution.py:24
  133.1 2.6 collective-permute-done.1
  135.7 21.3 %pad_maximum_fusion.2 = f32[4,80,18,1024]{3,2,1,0:T(8,128)} fusion(f32[4,80,1,1024]{3,2,1,0:T(1,128)} %collective-permute-done.1, f32[1,80,16,1024]{3,2,1,0:T(8,128)} %copy-done.3, f32[1,80,16,1024]{3,2,1,0:T(8,128)} %param.18, f32[1,80,16,1024]{3,2,1,0:T(8,128)} %param.17, f32[1,80,16,1024]{3,2,1,0:T(8,128)} %param.16, ...), kind=kLoop, calls=%fused_computation.42 | loop fusion | flops 29491200 | bytes 47185920 | tf_op jit(solution)/shard_map/concatenate | solution.py:26
  156.9 0.0 collective-permute-done.3
  156.9 2.9 fusion.30
  159.9 3.0 conditional.1
  159.9 3.0 broadcast.95
  162.9 0.8 slice.228
  163.8 2.8 gather_fusion.2
  166.6 1.3 collective-permute-start.4
  167.9 137.7 %collective-permute-done.4 = f32[1024,128]{1,0:T(8,128)} collective-permute-done((f32[1024,128]{1,0:T(8,128)S(1)}, f32[1024,128]{1,0:T(8,128)}, u32[]{:S(2)}, u32[]{:S(2)}) %collective-permute-start.4) | collective-permute-done | bytes 524320 | tf_op jit(solution)/shard_map/ppermute | solution.py:14
  305.6 9.2 %all-to-all-start.2 = ((f32[64,16,128]{2,1,0:T(8,128)}), f32[64,16,128]{2,1,0:T(8,128)S(1)}, u32[]{:S(2)}, u32[]{:S(2)}) async-start(f32[64,16,128]{2,1,0:T(8,128)} %bitcast.24), calls=%async_computation.2 | async-start | bytes 1048576 | tf_op jit(solution)/shard_map/all_to_all | solution.py:148
  314.8 0.0 copy-start.1
  314.8 3.5 %select_bitcast_fusion = f32[1,80,16,1024]{3,2,1,0:T(8,128)} fusion(f32[80,16,1024]{2,1,0:T(8,128)} %get-tuple-element.52, pred[]{:T(512)S(6)} %eq.43), kind=kLoop, calls=%fused_computation.43 | loop fusion | flops 1310720 | bytes 10485761 | tf_op jit(solution)/shard_map/broadcast_in_dim | solution.py:152
  318.3 9.9 %all-to-all-done.2 = f32[64,16,128]{2,1,0:T(8,128)S(1)} async-done(((f32[64,16,128]{2,1,0:T(8,128)}), f32[64,16,128]{2,1,0:T(8,128)S(1)}, u32[]{:S(2)}, u32[]{:S(2)}) %all-to-all-start.2) | async-done | bytes 524320 | tf_op jit(solution)/shard_map/all_to_all | solution.py:148
  328.2 1.0 gather_fusion.3
  329.2 0.7 select_bitcast_fusion.1
  (15 shorter events, 0.1 us)
Async XLA Ops:
  0.6 100.1 %copy-start = (f32[16,128]{1,0:T(8,128)S(1)}, f32[16,128]{1,0:T(8,128)}, u32[]{:S(2)}) copy-start(f32[16,128]{1,0:T(8,128)} %param.15) | copy-start | bytes 24580
  5.2 76.7 %copy-start.7 = (s32[1,16,1024]{2,1,0:T(8,128)S(1)}, s32[1,16,1024]{2,1,0:T(8,128)}, u32[]{:S(2)}) copy-start(s32[1,16,1024]{2,1,0:T(8,128)} %param.19) | copy-start | bytes 196612
  8.1 63.4 %all-to-all-start = ((s32[64,16,2]{1,2,0:T(2,128)}), s32[64,16,2]{1,2,0:T(2,128)S(1)}, u32[]{:S(2)}, u32[]{:S(2)}) async-start(s32[64,16,2]{1,2,0:T(2,128)} %copy.21), calls=%async_computation | async-start | bytes 131072 | tf_op jit(solution)/shard_map/all_to_all | solution.py:114
  71.5 39.5 %all-to-all-start.1 = ((f32[1024,4,128]{2,1,0:T(4,128)}), f32[1024,4,128]{2,1,0:T(4,128)S(1)}, u32[]{:S(2)}, u32[]{:S(2)}) async-start(f32[1024,4,128]{2,1,0:T(4,128)} %scatter_fusion), calls=%async_computation.1 | async-start | bytes 4194304 | tf_op jit(solution)/shard_map/all_to_all | solution.py:113
  82.5 10.0 %copy-start.3 = (f32[1,80,16,1024]{3,2,1,0:T(8,128)}, f32[1,80,16,1024]{3,2,1,0:T(8,128)S(1)}, u32[]{:S(2)}) copy-start(f32[1,80,16,1024]{3,2,1,0:T(8,128)S(1)} %fusion.23) | copy-start | bytes 15728644
  82.5 17.3 %slice-start = ((f32[1,80,16,1024]{3,2,1,0:T(8,128)}), f32[1,1,16,1024]{3,2,1,0:T(8,128)S(1)}, s32[]{:S(2)}) async-start(f32[1,80,16,1024]{3,2,1,0:T(8,128)} %param.16), calls=%async_computation.3 | async-start | bytes 131072 | tf_op jit(solution)/shard_map/slice | solution.py:106
  92.6 40.5 %collective-permute-start = (f32[4,80,1,1024]{3,2,1,0:T(1,128)}, f32[4,80,1,1024]{3,2,1,0:T(1,128)}, u32[]{:S(2)}, u32[]{:S(2)}) collective-permute-start(f32[4,80,1,1024]{3,2,1,0:T(1,128)} %get-tuple-element.47), channel_id=1, source_target_pairs={{0,1},{1,2},{2,3},{3,4},{4,5},{5,6},{6,7},{7,8},{8,9},{9,10},{10,1... | collective-permute-start | bytes 3932168 | tf_op jit(solution)/shard_map/ppermute | solution.py:24
  97.2 38.5 %collective-permute-start.1 = (f32[4,80,1,1024]{3,2,1,0:T(1,128)}, f32[4,80,1,1024]{3,2,1,0:T(1,128)}, u32[]{:S(2)}, u32[]{:S(2)}) collective-permute-start(f32[4,80,1,1024]{3,2,1,0:T(1,128)} %get-tuple-element.48), channel_id=1, source_target_pairs={{1,0},{2,1},{3,2},{4,3},{5,4},{6,5},{7,6},{8,7},{9,8},{10,9},{11,1... | collective-permute-start | bytes 3932168 | tf_op jit(solution)/shard_map/ppermute | solution.py:25
  98.6 2.1 collective-permute-start.2
  112.4 44.5 %collective-permute-start.3 = (f32[1024,4,128]{2,0,1:T(8,128)}, f32[1024,4,128]{2,0,1:T(8,128)}, u32[]{:S(2)}, u32[]{:S(2)}) collective-permute-start(f32[1024,4,128]{2,0,1:T(8,128)} %copy.23), channel_id=1, source_target_pairs={{0,64},{1,65},{2,66},{3,67},{4,68},{5,69},{6,70},{7,71},{8,72},{9,... | collective-permute-start | bytes 6291464 | tf_op jit(solution)/shard_map/ppermute | solution.py:14
  166.6 139.0 %collective-permute-start.4 = (f32[1024,128]{1,0:T(8,128)S(1)}, f32[1024,128]{1,0:T(8,128)}, u32[]{:S(2)}, u32[]{:S(2)}) collective-permute-start(f32[1024,128]{1,0:T(8,128)S(1)} %gather_fusion.2), channel_id=1, source_target_pairs={{64,0},{65,1},{66,2},{67,3},{68,4},{69,5},{70,6},{71,7},{72,8},{73... | collective-permute-start | bytes 1572872 | tf_op jit(solution)/shard_map/ppermute | solution.py:14
  305.6 22.6 %all-to-all-start.2 = ((f32[64,16,128]{2,1,0:T(8,128)}), f32[64,16,128]{2,1,0:T(8,128)S(1)}, u32[]{:S(2)}, u32[]{:S(2)}) async-start(f32[64,16,128]{2,1,0:T(8,128)} %bitcast.24), calls=%async_computation.2 | async-start | bytes 1048576 | tf_op jit(solution)/shard_map/all_to_all | solution.py:148
  314.8 15.2 %copy-start.1 = (f32[16,128]{1,0:T(8,128)S(1)}, f32[16,128]{1,0:T(8,128)}, u32[]{:S(2)}) copy-start(f32[16,128]{1,0:T(8,128)} %param.15) | copy-start | bytes 24580
where the time goes:
time: 333 us; the launch traced here: 330 us
  waiting for transfers between devices  172 us (52%)
  local copies, waits for them, and re-layouts  70.2 us (21%)
  starting transfers between devices  42.1 us (13%)
  other arithmetic  40.3 us (12%)
  matrix products  4.09 us (1%)
    ppermute x3, waiting for transfers between devices, passed_along(): lax.ppermute(value, axis, [(source, source + steps) for source in range(i...  138 us
    scatter x1, local copies, waits for them, and re-layouts, body(): packed = jnp.zeros((slot_count,) + atm_state.shape[2:], jnp.float32).at[p...  50.3 us
    concatenate x1, other arithmetic, extended(): array = jnp.concatenate([before, array, after], axis=dim)  21.3 us
    ppermute x1, waiting for transfers between devices, extended(): before = lax.ppermute(last, axis, up)  15.2 us
    all_to_all x1, starting transfers between devices, body(): lax.all_to_all(entries, 'tile', split_axis=0, concat_axis=0, tiled=True)  11.5 us
    all_to_all x1, starting transfers between devices, body(): lax.all_to_all(packed, 'tile', split_axis=0, concat_axis=0, tiled=True)  10.3 us
    slice x1, other arithmetic, extended(): last = lax.slice_in_dim(array, length - width, length, axis=dim)  10 us
    all_to_all x1, waiting for transfers between devices, body(): lax.all_to_all(received_patches, 'tile', split_axis=0, concat_axis=0, til...  9.91 us
  transfers between devices with their start and end apart: 8, of which 6 were waited for; matrix products, arithmetic and copies ran while one was open for 29% of the time, Pallas kernels for 0%

commit v1 on v0

v1 whole, which is shorter than its diff:
```python
import functools

import jax
import jax.numpy as jnp
from jax import lax
from jax.experimental import pallas as pl
from jax.experimental.pallas import tpu as pltpu
from jax.sharding import PartitionSpec as P

HEAT_DIFFUSION = 0.12
VERTICAL_MIXING = 0.2
FLUX_GAIN = 0.5
CAPACITY = 16
CHUNK = CAPACITY + 2
UNROLL = 8
LEVELS = 8

f32, bf16, i32 = jnp.float32, jnp.bfloat16, jnp.int32
VMEM = pl.BlockSpec(memory_space=pltpu.VMEM)
SMEM = pl.BlockSpec(memory_space=pltpu.SMEM)
ANY = pl.BlockSpec(memory_space=pl.ANY)


def iota(shape, axis):
    return lax.broadcasted_iota(i32, shape, axis)


def pack_kernel(
    tiles, sec, dest, block, row, state, depth, temp, merid,
    payload, slot_of, up, down,
    count, entry, edge, sem,
):
    levels = temp.shape[1]
    rows = temp.shape[2]

    @pl.when(sec[0] == 0)
    def _():
        def clear(i, _):
            count[i] = 0
            return 0

        lax.fori_loop(0, tiles, clear, 0)
        entry[...] = jnp.full(entry.shape, -1.0, f32)
        is_block = (iota((1, 128), 1) & 32) == 0

        def place(step, _):
            for j in range(UNROLL):
                i = step * UNROLL + j
                d = dest[i]
                c = count[d]
                count[d] = c + 1
                c = jnp.minimum(c, CAPACITY - 1)
                slot = d * CAPACITY + c
                slot_of[i] = slot
                payload[d * CHUNK + c] = state[0, i]
                entry[pl.ds(slot, 1), :] = jnp.where(is_block, block[i], row[i]).astype(f32)
            return 0

        lax.fori_loop(0, dest.shape[0] // UNROLL, place, 0)
        left = iota((8, 128), 1) < 64

        def entries_of(d, _):
            low = entry[pl.ds(pl.multiple_of(d * CAPACITY, 8), 8), :]
            high = entry[pl.ds(pl.multiple_of(d * CAPACITY + 8, 8), 8), :]
            both = jnp.where(left, low, high)
            payload[d * CHUNK + CAPACITY] = both[0:4]
            payload[d * CHUNK + CAPACITY + 1] = both[4:8]
            return 0

        lax.fori_loop(0, tiles, entries_of, 0)

    @pl.when(sec[0] != 0)
    def _():
        def none(i, _):
            slot_of[i] = 0
            return 0

        lax.fori_loop(0, dest.shape[0], none, 0)
        copies = []
        for n, (field, lo) in enumerate(
            ((temp, rows - 8), (merid, rows - 8), (temp, 0), (merid, 0))
        ):
            copies.append(
                pltpu.make_async_copy(field.at[0, :, pl.ds(lo, 8), :], edge.at[n], sem.at[n])
            )
        for copy in copies:
            copy.start()
        up[2 * levels :, :] = jnp.broadcast_to(
            depth[0, rows - 1 :, :].astype(f32), (8, depth.shape[2])
        )
        down[2 * levels :, :] = jnp.broadcast_to(
            depth[0, 0:1, :].astype(f32), (8, depth.shape[2])
        )
        for n, copy in enumerate(copies):
            copy.wait()
            target = up if n < 2 else down
            target[pl.ds((n % 2) * levels, levels), :] = edge[n, :, 7 if n < 2 else 0, :]


def ocean_kernel(
    levels, sec, temp, beneath, zonal, merid, depth, south, north,
    out, top,
    depth_e, depth_n, depth_s, carry,
):
    step = pl.program_id(0)
    rows, cells = depth.shape[1:]

    @pl.when(sec[0] == 0)
    def _():
        out[...] = jnp.zeros_like(out)

        @pl.when(step == 0)
        def _():
            top[...] = jnp.zeros_like(top)

    @pl.when(sec[0] != 0)
    def _():
        first = iota((rows, cells), 0) == 0
        last = iota((rows, cells), 0) == rows - 1

        @pl.when(step == 0)
        def _():
            d = depth[0]
            depth_e[...] = jnp.minimum(d, pltpu.roll(d, cells - 1, 1))
            d_north = north[2 * levels : 2 * levels + 1, :].astype(i32)
            d_south = south[2 * levels : 2 * levels + 1, :].astype(i32)
            depth_n[...] = jnp.minimum(d, jnp.where(last, d_north, pltpu.roll(d, rows - 1, 0)))
            depth_s[...] = jnp.broadcast_to(jnp.minimum(d[0:1], d_south), depth_s.shape)
            carry[...] = jnp.zeros_like(carry)

        above = carry[...]
        for j in range(LEVELS):
            k = step * LEVELS + j
            t = temp[0, j]
            u = zonal[0, j]
            v = merid[0, j]
            t_e = pltpu.roll(t, cells - 1, 1)
            u_e = pltpu.roll(u, cells - 1, 1)
            east = jnp.where(
                k < depth_e[...],
                HEAT_DIFFUSION * (t_e - t) - (0.25 * (u + u_e)) * (t + t_e),
                0.0,
            )
            t_n = jnp.where(last, north[pl.ds(k, 1), :], pltpu.roll(t, rows - 1, 0))
            v_n = jnp.where(last, north[pl.ds(levels + k, 1), :], pltpu.roll(v, rows - 1, 0))
            northward = jnp.where(
                k < depth_n[...],
                HEAT_DIFFUSION * (t_n - t) - (0.25 * (v + v_n)) * (t + t_n),
                0.0,
            )
            t_s = south[pl.ds(k, 1), :]
            v_s = south[pl.ds(levels + k, 1), :]
            t_0 = t[0:1]
            southmost = jnp.where(
                k < depth_s[0:1, :],
                HEAT_DIFFUSION * (t_0 - t_s) - (0.25 * (v[0:1] + v_s)) * (t_0 + t_s),
                0.0,
            )
            under = beneath[0, 0] if j == LEVELS - 1 else temp[0, j + 1]
            below = jnp.where(k + 1 < depth[0], VERTICAL_MIXING * (under - t), 0.0)
            fresh = (
                t
                + (east - pltpu.roll(east, 1, 1))
                + (northward - jnp.where(first, southmost, pltpu.roll(northward, 1, 0)))
                + (below - above)
            )
            above = below
            out[0, j] = fresh
            if j == 0:

                @pl.when(step == 0)
                def _():
                    wet = jnp.where(depth[0] > 0, FLUX_GAIN, 0.0)
                    patches = cells // 128
                    for p in range(patches):
                        part = slice(p * 128, p * 128 + 128)
                        top[0, pl.ds(p, rows, stride=patches), :] = t[:, part]
                        top[1, pl.ds(p, rows, stride=patches), :] = fresh[:, part]
                        top[2, pl.ds(p, rows, stride=patches), :] = wet[:, part]

        carry[...] = above


def in_three(x):
    high = x.astype(bf16)
    rest = x - high.astype(f32)
    middle = rest.astype(bf16)
    low = (rest - middle.astype(f32)).astype(bf16)
    return jnp.concatenate([high, middle, low], axis=1)


def joined(x, at=0):
    return x[:, at : at + 128] + (x[:, at + 128 : at + 256] + x[:, at + 256 : at + 384])


def heat_kernel(tiles, sec, payload, top, table, ret, fresh, hit, weighted):
    slots = tiles * CAPACITY

    @pl.when(sec[0] != 0)
    def _():
        ret[...] = jnp.zeros_like(ret)
        fresh[...] = jnp.zeros_like(fresh)

    @pl.when(sec[0] == 0)
    def _():
        surface_parts = in_three(top[0])
        table_parts = in_three(
            jnp.concatenate([table[...], jnp.zeros((128 - table.shape[0], 128), f32)], axis=0)
        )
        lane = iota((1, 8, 128), 2).astype(f32)
        group = 8

        def step(g, _):
            base = pl.multiple_of(g * group, group)
            upper = payload[pl.ds(base * CHUNK, group * CHUNK)].reshape(group, CHUNK, 4, 128)
            entry = upper[:, CAPACITY:].reshape(group, 8, 128)
            at = pl.multiple_of(base * CAPACITY, group * CAPACITY)
            size = group * CAPACITY
            block_hit = jnp.concatenate(
                [entry[:, None, :, 0:1] == lane[None], entry[:, None, :, 64:65] == lane[None]],
                axis=1,
            ).reshape(size, 128)
            row_hit = jnp.concatenate(
                [entry[:, None, :, 32:33] == lane[None], entry[:, None, :, 96:97] == lane[None]],
                axis=1,
            ).reshape(size, 128)
            live = jnp.concatenate(
                [
                    jnp.broadcast_to(entry[:, None, :, 0:1], (group, 1, 8, 128)),
                    jnp.broadcast_to(entry[:, None, :, 64:65], (group, 1, 8, 128)),
                ],
                axis=1,
            ).reshape(size, 128) >= 0
            block_one = jnp.where(block_hit, 1.0, 0.0).astype(bf16)
            row_one = jnp.where(row_hit, 1.0, 0.0).astype(bf16)
            hit[pl.ds(at, size), :] = block_one
            surface = joined(jnp.dot(block_one, surface_parts, preferred_element_type=f32))
            weights = joined(jnp.dot(row_one, table_parts, preferred_element_type=f32))

            def channel(c):
                return upper[:, :CAPACITY, c, :].reshape(size, 128)

            contrast = surface - channel(1)
            transfer = 0.8 + 0.4 * jnp.tanh(contrast)
            saturation = 0.6 * jnp.exp(0.3 * surface)
            heat = channel(3) - transfer * channel(0) * (
                contrast + 1.5 * (saturation - channel(2))
            )
            product = jnp.where(live, weights * heat, 0.0)
            weighted[pl.ds(at, size), 0:384] = in_three(product)
            weighted[pl.ds(at, size), 384:768] = in_three(weights)
            return 0

        lax.fori_loop(0, tiles // group, step, 0)
        sums = lax.dot_general(
            hit[...], weighted[...], (((0,), (0,)), ((), ())), preferred_element_type=f32
        )
        forcing = joined(sums) / jnp.maximum(joined(sums, 384), 1.0)
        new_top = top[1] + top[2] * forcing
        fresh[...] = new_top
        ret[...] = joined(jnp.dot(hit[...], in_three(new_top), preferred_element_type=f32))


def settle_kernel(fresh, whole, out):
    rows, cells = out.shape[2:]
    patches = cells // 128
    for p in range(patches):
        out[0, 0, :, p * 128 : p * 128 + 128] = fresh[pl.ds(p, rows, stride=patches), :]


def body(
    atm_state, routes, dst_block, weight_index, area_table, ocean_temp, vel_u, vel_v, depth_levels
):
    tiles = lax.axis_size("tile")
    block_count = atm_state.shape[1]
    levels, rows, cells = ocean_temp.shape[1:]
    patches = rows * cells // 128
    slots = tiles * CAPACITY
    sec = lax.axis_index("sec").astype(i32).reshape(1)
    grant = pltpu.CompilerParams(vmem_limit_bytes=48 << 20)

    edge_rows = 2 * levels + 8
    payload, slot_of, up, down = pl.pallas_call(
        functools.partial(pack_kernel, tiles),
        out_shape=(
            jax.ShapeDtypeStruct((tiles * CHUNK, 4, 128), f32),
            jax.ShapeDtypeStruct((block_count,), i32),
            jax.ShapeDtypeStruct((edge_rows, cells), f32),
            jax.ShapeDtypeStruct((edge_rows, cells), f32),
        ),
        in_specs=[SMEM, SMEM, SMEM, SMEM, VMEM, VMEM, ANY, ANY],
        out_specs=(VMEM, SMEM, VMEM, VMEM),
        scratch_shapes=[
            pltpu.SMEM((tiles,), i32),
            pltpu.VMEM((slots, 128), f32),
            pltpu.VMEM((4, levels, 8, cells), f32),
            pltpu.SemaphoreType.DMA((4,)),
        ],
        compiler_params=grant,
        name="pack",
    )(
        sec, routes.reshape(block_count), dst_block.reshape(block_count),
        weight_index.reshape(block_count), atm_state, depth_levels, ocean_temp, vel_v,
    )

    north_to = [(tiles + t, tiles + t + 1) for t in range(tiles - 1)]
    south_to = [(t + 1, t) for t in range(tiles, 2 * tiles - 1)]
    south = lax.ppermute(up, ("sec", "tile"), north_to)
    north = lax.ppermute(down, ("sec", "tile"), south_to)
    moved = lax.all_to_all(payload, "tile", split_axis=0, concat_axis=0, tiled=True)

    steps = levels // LEVELS
    slab = pl.BlockSpec((1, LEVELS, rows, cells), lambda i: (0, i, 0, 0))
    fixed3 = pl.BlockSpec((1, rows, cells), lambda i: (0, 0, 0))
    fixed2 = pl.BlockSpec((edge_rows, cells), lambda i: (0, 0))
    out, top = pl.pallas_call(
        functools.partial(ocean_kernel, levels),
        grid=(steps,),
        out_shape=(
            jax.ShapeDtypeStruct(ocean_temp.shape, f32),
            jax.ShapeDtypeStruct((3, patches, 128), f32),
        ),
        in_specs=[
            SMEM,
            slab,
            pl.BlockSpec(
                (1, 1, rows, cells),
                lambda i: (0, jnp.minimum((i + 1) * LEVELS, levels - 1), 0, 0),
            ),
            slab,
            slab,
            fixed3,
            fixed2,
            fixed2,
        ],
        out_specs=(slab, pl.BlockSpec((3, patches, 128), lambda i: (0, 0, 0))),
        scratch_shapes=[
            pltpu.VMEM((rows, cells), i32),
            pltpu.VMEM((rows, cells), i32),
            pltpu.VMEM((8, cells), i32),
            pltpu.VMEM((rows, cells), f32),
        ],
        compiler_params=grant,
        cost_estimate=pl.CostEstimate(
            flops=40 * levels * rows * cells,
            bytes_accessed=17 * levels * rows * cells,
            transcendentals=0,
        ),
        name="ocean",
    )(sec, ocean_temp, ocean_temp, vel_u, vel_v, depth_levels, south, north)
    top = lax.ppermute(top, "sec", [(1, 0)])

    ret, fresh = pl.pallas_call(
        functools.partial(heat_kernel, tiles),
        out_shape=(
            jax.ShapeDtypeStruct((slots, 128), f32),
            jax.ShapeDtypeStruct((patches, 128), f32),
        ),
        in_specs=[SMEM, VMEM, VMEM, VMEM],
        out_specs=(VMEM, VMEM),
        scratch_shapes=[pltpu.VMEM((slots, 128), bf16), pltpu.VMEM((slots, 768), bf16)],
        compiler_params=grant,
        name="heat",
    )(sec, moved, top, area_table)

    fresh = lax.ppermute(fresh, "sec", [(0, 1)])
    back = lax.all_to_all(ret, "tile", split_axis=0, concat_axis=0, tiled=True)
    level = pl.BlockSpec((1, 1, rows, cells), lambda i: (0, 0, 0, 0))
    following = pl.pallas_call(
        settle_kernel,
        grid=(1,),
        out_shape=jax.ShapeDtypeStruct(out.shape, f32),
        in_specs=[pl.BlockSpec((patches, 128), lambda i: (0, 0)), ANY],
        out_specs=level,
        input_output_aliases={1: 0},
        name="settle",
    )(fresh, out)
    skin = back.at[slot_of].get(mode="promise_in_bounds")
    return following, skin[None]


def solution(mesh):
    return jax.shard_map(
        body,
        mesh=mesh,
        in_specs=(
            P("sec", "tile", None, None),
            P("sec", "tile", None),
            P("sec", "tile"),
            P("sec", "tile"),
            P(),
            P("sec", None, "tile", None),
            P("sec", None, "tile", None),
            P("sec", None, "tile", None),
            P("sec", "tile", None),
        ),
        out_specs=(P("sec", None, "tile", None), P("sec", "tile", None)),
        check_vma=False,
    )
```

time: 333 us -> 106 us (0.32)
  waiting for transfers between devices: 172 us -> 49.5 us
  local copies, waits for them, and re-layouts: 70.2 us -> 8.64 us
  other arithmetic: 40.3 us -> 0.01 us
  Pallas kernels: 0 us -> 21.2 us
  starting transfers between devices: 42.1 us -> 25.2 us
  matrix products: 4.09 us -> 0 us
    ppermute x5 -> x4, waiting for transfers between devices: 156 us -> 42.1 us  [the longest x1 41.2 us: body(): top = lax.ppermute(top, 'sec', [(1, 0)])]
    scatter x2 -> x0, local copies, waits for them, and re-layouts: 52.1 us -> none  [the longest x1 50.3 us: body(): packed = jnp.zeros((slot_count,) + atm_state.shape[2:], jnp.float32).at[p...]
    concatenate x1 -> x0, other arithmetic: 21.3 us -> none  [extended(): array = jnp.concatenate([before, array, after], axis=dim)]
    pallas_call x0 -> x4, Pallas kernels: none -> 21.2 us  [the longest x1 10.1 us: body(): pl.pallas_call(functools.partial(ocean_kernel, levels), grid=(steps,), ou...]
    slice x1 -> x0, other arithmetic: 10 us -> none  [extended(): last = lax.slice_in_dim(array, length - width, length, axis=dim)]
    all_to_all x3 -> x2, starting transfers between devices: 31 us -> 21.2 us  [the longest x1 11.5 us: body(): lax.all_to_all(payload, 'tile', split_axis=0, concat_axis=0, tiled=True)]
    all_to_all x3 -> x2, waiting for transfers between devices: 16.2 us -> 7.4 us  [the longest x1 7.4 us: body(): back = lax.all_to_all(ret, 'tile', split_axis=0, concat_axis=0, tiled=True)]
    gather x4 -> x1, local copies, waits for them, and re-layouts: 9.47 us -> 1.64 us  [body(): skin = back.at[slot_of].get(mode='promise_in_bounds')]
  transfers between devices with their start and end apart: 8 -> 6, of which waited for: 6 -> 3; matrix products, arithmetic and copies ran while one was open for 29% -> 0% of each run, Pallas kernels for 0% -> 11%
where the time goes in v1:
time: 106 us; the launch traced here: 105 us
  waiting for transfers between devices  49.5 us (47%)
  starting transfers between devices  25.2 us (24%)
  Pallas kernels  21.2 us (20%)
  local copies, waits for them, and re-layouts  8.64 us (8%)
    ppermute x1, waiting for transfers between devices, body(): top = lax.ppermute(top, 'sec', [(1, 0)])  41.2 us
    all_to_all x1, starting transfers between devices, body(): lax.all_to_all(payload, 'tile', split_axis=0, concat_axis=0, tiled=True)  11.5 us
    pallas_call x1, Pallas kernels, body(): pl.pallas_call(functools.partial(ocean_kernel, levels), grid=(steps,), ou...  10.1 us
    all_to_all x1, starting transfers between devices, body(): back = lax.all_to_all(ret, 'tile', split_axis=0, concat_axis=0, tiled=True)  9.73 us
    all_to_all x1, waiting for transfers between devices, body(): back = lax.all_to_all(ret, 'tile', split_axis=0, concat_axis=0, tiled=True)  7.4 us
    unnamed x20, local copies, waits for them, and re-layouts  7 us
    pallas_call x1, Pallas kernels, body(): pl.pallas_call(functools.partial(pack_kernel, tiles), out_shape=(jax.Shap...  4.96 us
    pallas_call x1, Pallas kernels, body(): pl.pallas_call(functools.partial(heat_kernel, tiles), out_shape=(jax.Shap...  4.66 us
  transfers between devices with their start and end apart: 6, of which 3 were waited for; matrix products, arithmetic and copies ran while one was open for 0% of the time, Pallas kernels for 11%

profile of v1, /device:TPU:0, one launch (start us, length us, event | category | flops | bytes accessed | tf_op | source)
XLA Modules:
  0.0 105.3 jit_solution(7407794333911052620)
XLA Ops:
  0.6 0.0 copy-start.1
  0.6 1.2 %copy-done.1 = f32[1,512,4,128]{3,2,1,0:T(4,128)S(1)} copy-done((f32[1,512,4,128]{3,2,1,0:T(4,128)S(1)}, f32[1,512,4,128]{3,2,1,0:T(4,128)}, u32[]{:S(2)}) %copy-start.1) | copy-done | bytes 1048600
  1.9 0.0 copy-start.2
  1.9 0.8 copy-done.2
  2.7 0.0 copy-start.5
  2.7 0.7 copy-done.5
  3.4 0.0 copy-start.6
  3.4 0.7 copy-done.6
  4.1 0.0 copy-start.7
  4.1 0.7 copy-done.7
  4.7 0.0 copy-start.3
  4.8 5.0 %pack.1 = (f32[1152,4,128]{2,1,0:T(4,128)S(1)}, s32[512]{0:T(512)S(1)}, f32[168,1024]{1,0:T(8,128)S(1)}, f32[168,1024]{1,0:T(8,128)S(1)}) custom-call(s32[1]{0:T(128)} %bitcast.sec, s32[512]{0:T(512)S(1)} %bitcast.7, s32[512]{0:T(512)S(1)} %bitcast.8, s32[512]{0:T(512)S(1)} %bitcast.9, f32[1,512,4,128]{3,2,1,0:T(4,128)S(1)} %copy-done.1, ...), custom_call_target="tpu_custom_call" | custom-call | tf_op jit(solution)/shard_map/pack/pallas_call | solution.py:283
  9.7 0.0 copy-start
  9.7 1.4 %copy-done = f32[1152,4,128]{2,1,0:T(4,128)} copy-done((f32[1152,4,128]{2,1,0:T(4,128)}, f32[1152,4,128]{2,1,0:T(4,128)S(1)}, u32[]{:S(2)}) %copy-start) | copy-done | bytes 2359320
  11.1 0.0 copy-start.8
  11.1 0.8 copy-done.8
  12.0 11.5 %all-to-all-start = ((f32[1152,4,128]{2,1,0:T(4,128)}), f32[1152,4,128]{2,1,0:T(4,128)S(1)}, u32[]{:S(2)}, u32[]{:S(2)}) async-start(f32[1152,4,128]{2,1,0:T(4,128)} %copy-done), calls=%async_computation | async-start | bytes 4718592 | tf_op jit(solution)/shard_map/all_to_all | solution.py:310
  23.5 0.7 collective-permute-start
  24.2 0.0 copy-start.4
  24.2 0.7 collective-permute-start.1
  24.9 0.0 collective-permute-done.south
  24.9 0.0 collective-permute-done.1.north
  25.0 0.0 copy-done.3
  25.0 10.1 %ocean.1 = (f32[1,80,16,1024]{3,2,1,0:T(8,128)}, f32[3,128,128]{2,1,0:T(8,128)S(1)}) custom-call(s32[1]{0:T(128)} %bitcast.sec, f32[1,80,16,1024]{3,2,1,0:T(8,128)} %beneath.1, f32[1,80,16,1024]{3,2,1,0:T(8,128)} %beneath.1, f32[1,80,16,1024]{3,2,1,0:T(8,128)} %zonal.1, f32[1,80,16,1024]{3,2,1,0:T(8,128)} %merid.3, s32[1,16,1024]{2,1,0:T(8,128)S(1)} %copy-done.3, ...), custom_call_target="tpu_custom_call" | custom-call | flops 52428800 | bytes 22282240 | tf_op jit(solution)/shard_map/ocean/pallas_call | solution.py:316
  35.0 1.3 %collective-permute-start.2 = (f32[3,128,128]{2,1,0:T(8,128)S(1)}, f32[3,128,128]{2,1,0:T(8,128)S(1)}, u32[]{:S(2)}, u32[]{:S(2)}) collective-permute-start(f32[3,128,128]{2,1,0:T(8,128)S(1)} %get-tuple-element.13), channel_id=1, source_target_pairs={{64,0},{65,1},{66,2},{67,3},{68,4},{69,5},{70,6},{71,7},{72,8},{73... | collective-permute-start | bytes 589832 | tf_op jit(solution)/shard_map/ppermute | solution.py:351
  36.3 41.2 %collective-permute-done.2.top = f32[3,128,128]{2,1,0:T(8,128)S(1)} collective-permute-done((f32[3,128,128]{2,1,0:T(8,128)S(1)}, f32[3,128,128]{2,1,0:T(8,128)S(1)}, u32[]{:S(2)}, u32[]{:S(2)}) %collective-permute-start.2) | collective-permute-done | bytes 196640 | tf_op jit(solution)/shard_map/ppermute | solution.py:351
  77.5 0.0 all-to-all-done.payload
  77.5 0.0 copy-done.4
  77.5 4.7 %heat.1 = (f32[1024,128]{1,0:T(8,128)}, f32[128,128]{1,0:T(8,128)S(1)}) custom-call(s32[1]{0:T(128)} %bitcast.sec, f32[1152,4,128]{2,1,0:T(4,128)S(1)} %all-to-all-done.payload, f32[3,128,128]{2,1,0:T(8,128)S(1)} %collective-permute-done.2.top, f32[16,128]{1,0:T(8,128)S(1)} %copy-done.4), custom_call_target="tpu_custom_call" | custom-call | tf_op jit(solution)/shard_map/heat/pallas_call | solution.py:353
  82.2 9.7 %all-to-all-start.1 = ((f32[64,16,128]{2,1,0:T(8,128)}), f32[64,16,128]{2,1,0:T(8,128)S(1)}, u32[]{:S(2)}, u32[]{:S(2)}) async-start(f32[64,16,128]{2,1,0:T(8,128)} %bitcast.4), calls=%async_computation.1 | async-start | bytes 1048576 | tf_op jit(solution)/shard_map/all_to_all | solution.py:367
  92.0 1.3 %collective-permute-start.3 = (f32[128,128]{1,0:T(8,128)S(1)}, f32[128,128]{1,0:T(8,128)S(1)}, u32[]{:S(2)}, u32[]{:S(2)}) collective-permute-start(f32[128,128]{1,0:T(8,128)S(1)} %get-tuple-element.14), channel_id=1, source_target_pairs={{0,64},{1,65},{2,66},{3,67},{4,68},{5,69},{6,70},{7,71},{8,72},{9,... | collective-permute-start | bytes 196616 | tf_op jit(solution)/shard_map/ppermute | solution.py:366
  93.3 0.9 collective-permute-done.3.fresh
  94.1 0.0 copy-start.9
  94.1 0.6 copy-done.9
  94.8 1.5 %settle.1 = f32[1,80,16,1024]{3,2,1,0:T(8,128)} custom-call(f32[128,128]{1,0:T(8,128)} %copy-done.9, f32[1,80,16,1024]{3,2,1,0:T(8,128)} %get-tuple-element.15.whole), custom_call_target="tpu_custom_call", output_to_operand_aliasing={{}: (1, {})} | custom-call | tf_op jit(solution)/shard_map/settle/pallas_call | solution.py:369
  96.2 7.4 %all-to-all-done.1 = f32[64,16,128]{2,1,0:T(8,128)S(1)} async-done(((f32[64,16,128]{2,1,0:T(8,128)}), f32[64,16,128]{2,1,0:T(8,128)S(1)}, u32[]{:S(2)}, u32[]{:S(2)}) %all-to-all-start.1) | async-done | bytes 524320 | tf_op jit(solution)/shard_map/all_to_all | solution.py:367
  103.6 1.6 %gather_fusion = f32[512,128]{1,0:T(8,128)} fusion(f32[1024,128]{1,0:T(8,128)S(1)} %bitcast.10, s32[1024]{0:T(1024)S(1)} %pad_clamp_fusion), kind=kCustom, calls=%fused_computation | custom fusion | bytes 526336 | tf_op jit(solution)/shard_map/gather | solution.py:378
  (2 shorter events, 0.0 us)
Async XLA Ops:
  0.6 1.2 %copy-start.1 = (f32[1,512,4,128]{3,2,1,0:T(4,128)S(1)}, f32[1,512,4,128]{3,2,1,0:T(4,128)}, u32[]{:S(2)}) copy-start(f32[1,512,4,128]{3,2,1,0:T(4,128)} %state.1) | copy-start | bytes 3145732
  1.9 0.8 copy-start.2
  2.7 0.7 copy-start.5
  3.4 0.7 copy-start.6
  4.1 0.7 copy-start.7
  4.7 20.2 %copy-start.3 = (s32[1,16,1024]{2,1,0:T(8,128)S(1)}, s32[1,16,1024]{2,1,0:T(8,128)}, u32[]{:S(2)}) copy-start(s32[1,16,1024]{2,1,0:T(8,128)} %depth.3) | copy-start | bytes 196612
  9.7 1.4 %copy-start = (f32[1152,4,128]{2,1,0:T(4,128)}, f32[1152,4,128]{2,1,0:T(4,128)S(1)}, u32[]{:S(2)}) copy-start(f32[1152,4,128]{2,1,0:T(4,128)S(1)} %get-tuple-element.10) | copy-start | bytes 7077892
  11.1 0.8 copy-start.8
  12.0 65.5 %all-to-all-start = ((f32[1152,4,128]{2,1,0:T(4,128)}), f32[1152,4,128]{2,1,0:T(4,128)S(1)}, u32[]{:S(2)}, u32[]{:S(2)}) async-start(f32[1152,4,128]{2,1,0:T(4,128)} %copy-done), calls=%async_computation | async-start | bytes 4718592 | tf_op jit(solution)/shard_map/all_to_all | solution.py:310
  23.5 1.4 %collective-permute-start = (f32[168,1024]{1,0:T(8,128)}, f32[168,1024]{1,0:T(8,128)S(1)}, u32[]{:S(2)}, u32[]{:S(2)}) collective-permute-start(f32[168,1024]{1,0:T(8,128)} %copy-done.8), channel_id=1, source_target_pairs={{64,65},{65,66},{66,67},{67,68},{68,69},{69,70},{70,71},{71,72},{7... | collective-permute-start | bytes 2064392 | tf_op jit(solution)/shard_map/ppermute | solution.py:308
  24.2 53.3 %copy-start.4 = (f32[16,128]{1,0:T(8,128)S(1)}, f32[16,128]{1,0:T(8,128)}, u32[]{:S(2)}) copy-start(f32[16,128]{1,0:T(8,128)} %table.1) | copy-start | bytes 24580
  24.2 0.7 collective-permute-start.1
  35.0 42.5 %collective-permute-start.2 = (f32[3,128,128]{2,1,0:T(8,128)S(1)}, f32[3,128,128]{2,1,0:T(8,128)S(1)}, u32[]{:S(2)}, u32[]{:S(2)}) collective-permute-start(f32[3,128,128]{2,1,0:T(8,128)S(1)} %get-tuple-element.13), channel_id=1, source_target_pairs={{64,0},{65,1},{66,2},{67,3},{68,4},{69,5},{70,6},{71,7},{72,8},{73... | collective-permute-start | bytes 589832 | tf_op jit(solution)/shard_map/ppermute | solution.py:351
  82.2 21.4 %all-to-all-start.1 = ((f32[64,16,128]{2,1,0:T(8,128)}), f32[64,16,128]{2,1,0:T(8,128)S(1)}, u32[]{:S(2)}, u32[]{:S(2)}) async-start(f32[64,16,128]{2,1,0:T(8,128)} %bitcast.4), calls=%async_computation.1 | async-start | bytes 1048576 | tf_op jit(solution)/shard_map/all_to_all | solution.py:367
  92.0 2.2 %collective-permute-start.3 = (f32[128,128]{1,0:T(8,128)S(1)}, f32[128,128]{1,0:T(8,128)S(1)}, u32[]{:S(2)}, u32[]{:S(2)}) collective-permute-start(f32[128,128]{1,0:T(8,128)S(1)} %get-tuple-element.14), channel_id=1, source_target_pairs={{0,64},{1,65},{2,66},{3,67},{4,68},{5,69},{6,70},{7,71},{8,72},{9,... | collective-permute-start | bytes 196616 | tf_op jit(solution)/shard_map/ppermute | solution.py:366
  94.1 0.6 copy-start.9

commit v2 on v1

v2 whole, which is shorter than its diff:
```python
import functools

import jax
import jax.numpy as jnp
from jax import lax
from jax.experimental import pallas as pl
from jax.experimental.pallas import tpu as pltpu
from jax.sharding import PartitionSpec as P

HEAT_DIFFUSION = 0.12
VERTICAL_MIXING = 0.2
FLUX_GAIN = 0.5
CAPACITY = 16
CHUNK = CAPACITY + 2
UNROLL = 8
LEVELS = 8

f32, bf16, i32 = jnp.float32, jnp.bfloat16, jnp.int32
VMEM = pl.BlockSpec(memory_space=pltpu.VMEM)
SMEM = pl.BlockSpec(memory_space=pltpu.SMEM)
ANY = pl.BlockSpec(memory_space=pl.ANY)
HBM = pl.BlockSpec(memory_space=pltpu.HBM)


def iota(shape, axis):
    return lax.broadcasted_iota(i32, shape, axis)


def pack_kernel(
    tiles, sec, dest_in, block_in, row_in, state_in, depth_in, temp, merid,
    payload_out, slot_of, up_out, down_out,
    dest, block, row, state, payload, count, entry, edge, depth, up, down,
    index_sem, state_sem, edge_sem, out_sem,
):
    levels = temp.shape[1]
    rows = temp.shape[2]
    blocks = dest.shape[0]
    pieces = state_sem.shape[0]
    piece = blocks // pieces

    @pl.when(sec[0] == 0)
    def _():
        indices = [
            pltpu.make_async_copy(source, target, index_sem.at[n])
            for n, (source, target) in enumerate(
                ((dest_in, dest), (block_in, block), (row_in, row))
            )
        ]
        states = [
            pltpu.make_async_copy(
                state_in.at[0, pl.ds(n * piece, piece)],
                state.at[pl.ds(n * piece, piece)],
                state_sem.at[n],
            )
            for n in range(pieces)
        ]
        for copy in indices + states:
            copy.start()

        for i in range(tiles):
            count[i] = 0
        entry[...] = jnp.full(entry.shape, -1.0, f32)
        is_block = (iota((1, 128), 1) & 32) == 0
        for copy in indices:
            copy.wait()

        def place(step, _):
            for j in range(UNROLL):
                i = step * UNROLL + j
                d = dest[i]
                c = count[d]
                count[d] = c + 1
                c = jnp.minimum(c, CAPACITY - 1)
                slot = d * CAPACITY + c
                slot_of[i] = slot
                payload[d * CHUNK + c] = state[i]
                entry[pl.ds(slot, 1), :] = jnp.where(is_block, block[i], row[i]).astype(f32)
            return 0

        for n in range(pieces):
            states[n].wait()
            lax.fori_loop(n * piece // UNROLL, (n + 1) * piece // UNROLL, place, 0)
        left = iota((8, 128), 1) < 64

        def entries_of(g, _):
            for j in range(8):
                d = g * 8 + j
                low = entry[pl.ds(pl.multiple_of(d * CAPACITY, 8), 8), :]
                high = entry[pl.ds(pl.multiple_of(d * CAPACITY + 8, 8), 8), :]
                both = jnp.where(left, low, high)
                payload[d * CHUNK + CAPACITY] = both[0:4]
                payload[d * CHUNK + CAPACITY + 1] = both[4:8]
            return 0

        lax.fori_loop(0, tiles // 8, entries_of, 0)
        half = payload.shape[0] // 2
        outs = [
            pltpu.make_async_copy(
                payload.at[pl.ds(n * half, half)], payload_out.at[pl.ds(n * half, half)], out_sem.at[n]
            )
            for n in range(2)
        ]
        for copy in outs:
            copy.start()
        for copy in outs:
            copy.wait()

    @pl.when(sec[0] != 0)
    def _():
        bring = pltpu.make_async_copy(depth_in.at[0], depth, index_sem.at[0])
        bring.start()
        copies = [
            pltpu.make_async_copy(field.at[0, :, pl.ds(lo, 8), :], edge.at[n], edge_sem.at[n])
            for n, (field, lo) in enumerate(
                ((temp, rows - 8), (merid, rows - 8), (temp, 0), (merid, 0))
            )
        ]
        for copy in copies:
            copy.start()

        def none(step, _):
            for j in range(UNROLL):
                slot_of[step * UNROLL + j] = 0
            return 0

        lax.fori_loop(0, blocks // UNROLL, none, 0)
        bring.wait()
        cells = depth.shape[1]
        up[2 * levels :, :] = jnp.broadcast_to(depth[rows - 1 :, :].astype(f32), (8, cells))
        down[2 * levels :, :] = jnp.broadcast_to(depth[0:1, :].astype(f32), (8, cells))
        for n, copy in enumerate(copies):
            copy.wait()
            target = up if n < 2 else down
            target[pl.ds((n % 2) * levels, levels), :] = edge[n, :, 7 if n < 2 else 0, :]
        outs = [
            pltpu.make_async_copy(up, up_out, out_sem.at[0]),
            pltpu.make_async_copy(down, down_out, out_sem.at[1]),
        ]
        for copy in outs:
            copy.start()
        for copy in outs:
            copy.wait()


def faces(levels, k, t, u, v, north, south, depth_e, depth_n, depth_s):
    rows, cells = t.shape
    first = iota((rows, cells), 0) == 0
    last = iota((rows, cells), 0) == rows - 1
    t_e = pltpu.roll(t, cells - 1, 1)
    u_e = pltpu.roll(u, cells - 1, 1)
    east = jnp.where(
        k < depth_e,
        HEAT_DIFFUSION * (t_e - t) - (0.25 * (u + u_e)) * (t + t_e),
        0.0,
    )
    t_n = jnp.where(last, north[pl.ds(k, 1), :], pltpu.roll(t, rows - 1, 0))
    v_n = jnp.where(last, north[pl.ds(levels + k, 1), :], pltpu.roll(v, rows - 1, 0))
    northward = jnp.where(
        k < depth_n,
        HEAT_DIFFUSION * (t_n - t) - (0.25 * (v + v_n)) * (t + t_n),
        0.0,
    )
    t_s = south[pl.ds(k, 1), :]
    v_s = south[pl.ds(levels + k, 1), :]
    t_0 = t[0:1]
    southmost = jnp.where(
        k < depth_s,
        HEAT_DIFFUSION * (t_0 - t_s) - (0.25 * (v[0:1] + v_s)) * (t_0 + t_s),
        0.0,
    )
    return (east - pltpu.roll(east, 1, 1)) + (
        northward - jnp.where(first, southmost, pltpu.roll(northward, 1, 0))
    )


def face_depths(levels, d, north, south):
    rows, cells = d.shape
    last = iota((rows, cells), 0) == rows - 1
    d_north = north[2 * levels : 2 * levels + 1, :].astype(i32)
    d_south = south[2 * levels : 2 * levels + 1, :].astype(i32)
    return (
        jnp.minimum(d, pltpu.roll(d, cells - 1, 1)),
        jnp.minimum(d, jnp.where(last, d_north, pltpu.roll(d, rows - 1, 0))),
        jnp.minimum(d[0:1], d_south),
    )


def surface_kernel(levels, sec, temp, zonal, merid, depth, south, north, top):
    @pl.when(sec[0] != 0)
    def _():
        d = depth[0]
        rows, cells = d.shape
        t = temp[0, 0]
        below = jnp.where(1 < d, VERTICAL_MIXING * (temp[0, 1] - t), 0.0)
        base = t + faces(
            levels, 0, t, zonal[0, 0], merid[0, 0], north, south,
            *face_depths(levels, d, north, south),
        ) + below
        wet = jnp.where(d > 0, FLUX_GAIN, 0.0)
        patches = cells // 128
        for p in range(patches):
            part = slice(p * 128, p * 128 + 128)
            top[0, pl.ds(p, rows, stride=patches), :] = t[:, part]
            top[1, pl.ds(p, rows, stride=patches), :] = base[:, part]
            top[2, pl.ds(p, rows, stride=patches), :] = wet[:, part]


def ocean_kernel(
    levels, sec, temp, beneath, zonal, merid, depth, south, north,
    out,
    depth_e, depth_n, depth_s, carry,
):
    step = pl.program_id(0)

    @pl.when(sec[0] == 0)
    def _():
        out[...] = jnp.zeros_like(out)

    @pl.when(sec[0] != 0)
    def _():
        @pl.when(step == 0)
        def _():
            e, n, s = face_depths(levels, depth[0], north, south)
            depth_e[...] = e
            depth_n[...] = n
            depth_s[...] = jnp.broadcast_to(s, depth_s.shape)
            carry[...] = jnp.zeros_like(carry)

        above = carry[...]
        for j in range(LEVELS):
            k = step * LEVELS + j
            t = temp[0, j]
            under = beneath[0, 0] if j == LEVELS - 1 else temp[0, j + 1]
            below = jnp.where(k + 1 < depth[0], VERTICAL_MIXING * (under - t), 0.0)
            out[0, j] = (
                t
                + faces(
                    levels, k, t, zonal[0, j], merid[0, j], north, south,
                    depth_e[...], depth_n[...], depth_s[0:1, :],
                )
                + (below - above)
            )
            above = below
        carry[...] = above


def in_three(x):
    high = x.astype(bf16)
    rest = x - high.astype(f32)
    middle = rest.astype(bf16)
    low = (rest - middle.astype(f32)).astype(bf16)
    return jnp.concatenate([high, middle, low], axis=1)


def joined(x, at=0):
    return x[:, at : at + 128] + (x[:, at + 128 : at + 256] + x[:, at + 256 : at + 384])


def heat_kernel(tiles, sec, payload, top, table, ret, fresh, hit, weighted):
    slots = tiles * CAPACITY

    @pl.when(sec[0] != 0)
    def _():
        ret[...] = jnp.zeros_like(ret)
        fresh[...] = jnp.zeros_like(fresh)

    @pl.when(sec[0] == 0)
    def _():
        surface_parts = in_three(top[0])
        table_parts = in_three(
            jnp.concatenate([table[...], jnp.zeros((128 - table.shape[0], 128), f32)], axis=0)
        )
        lane = iota((1, 8, 128), 2).astype(f32)
        group = 8

        def step(g, _):
            base = pl.multiple_of(g * group, group)
            upper = payload[pl.ds(base * CHUNK, group * CHUNK)].reshape(group, CHUNK, 4, 128)
            entry = upper[:, CAPACITY:].reshape(group, 8, 128)
            at = pl.multiple_of(base * CAPACITY, group * CAPACITY)
            size = group * CAPACITY
            block_hit = jnp.concatenate(
                [entry[:, None, :, 0:1] == lane[None], entry[:, None, :, 64:65] == lane[None]],
                axis=1,
            ).reshape(size, 128)
            row_hit = jnp.concatenate(
                [entry[:, None, :, 32:33] == lane[None], entry[:, None, :, 96:97] == lane[None]],
                axis=1,
            ).reshape(size, 128)
            live = jnp.concatenate(
                [
                    jnp.broadcast_to(entry[:, None, :, 0:1], (group, 1, 8, 128)),
                    jnp.broadcast_to(entry[:, None, :, 64:65], (group, 1, 8, 128)),
                ],
                axis=1,
            ).reshape(size, 128) >= 0
            block_one = jnp.where(block_hit, 1.0, 0.0).astype(bf16)
            row_one = jnp.where(row_hit, 1.0, 0.0).astype(bf16)
            hit[pl.ds(at, size), :] = block_one
            surface = joined(jnp.dot(block_one, surface_parts, preferred_element_type=f32))
            weights = joined(jnp.dot(row_one, table_parts, preferred_element_type=f32))

            def channel(c):
                return upper[:, :CAPACITY, c, :].reshape(size, 128)

            contrast = surface - channel(1)
            transfer = 0.8 + 0.4 * jnp.tanh(contrast)
            saturation = 0.6 * jnp.exp(0.3 * surface)
            heat = channel(3) - transfer * channel(0) * (
                contrast + 1.5 * (saturation - channel(2))
            )
            product = jnp.where(live, weights * heat, 0.0)
            weighted[pl.ds(at, size), 0:384] = in_three(product)
            weighted[pl.ds(at, size), 384:768] = in_three(weights)
            return 0

        lax.fori_loop(0, tiles // group, step, 0)
        sums = lax.dot_general(
            hit[...], weighted[...], (((0,), (0,)), ((), ())), preferred_element_type=f32
        )
        forcing = joined(sums) / jnp.maximum(joined(sums, 384), 1.0)
        new_top = top[1] + top[2] * forcing
        fresh[...] = new_top
        ret[...] = joined(jnp.dot(hit[...], in_three(new_top), preferred_element_type=f32))


def settle_kernel(fresh, whole, out):
    rows, cells = out.shape[2:]
    patches = cells // 128
    for p in range(patches):
        out[0, 0, :, p * 128 : p * 128 + 128] = fresh[pl.ds(p, rows, stride=patches), :]


def body(
    atm_state, routes, dst_block, weight_index, area_table, ocean_temp, vel_u, vel_v, depth_levels
):
    tiles = lax.axis_size("tile")
    block_count = atm_state.shape[1]
    levels, rows, cells = ocean_temp.shape[1:]
    patches = rows * cells // 128
    slots = tiles * CAPACITY
    sec = lax.axis_index("sec").astype(i32).reshape(1)
    grant = pltpu.CompilerParams(vmem_limit_bytes=24 << 20)
    ocean_grant = pltpu.CompilerParams(vmem_limit_bytes=56 << 20)
    whole_grant = pltpu.CompilerParams(vmem_limit_bytes=60 << 20)

    edge_rows = 2 * levels + 8
    payload, slot_of, up, down = pl.pallas_call(
        functools.partial(pack_kernel, tiles),
        out_shape=(
            jax.ShapeDtypeStruct((tiles * CHUNK, 4, 128), f32),
            jax.ShapeDtypeStruct((block_count,), i32),
            jax.ShapeDtypeStruct((edge_rows, cells), f32),
            jax.ShapeDtypeStruct((edge_rows, cells), f32),
        ),
        in_specs=[SMEM] + [HBM] * 7,
        out_specs=(HBM, SMEM, HBM, HBM),
        scratch_shapes=[
            pltpu.SMEM((block_count,), i32),
            pltpu.SMEM((block_count,), i32),
            pltpu.SMEM((block_count,), i32),
            pltpu.VMEM((block_count, 4, 128), f32),
            pltpu.VMEM((tiles * CHUNK, 4, 128), f32),
            pltpu.SMEM((tiles,), i32),
            pltpu.VMEM((slots, 128), f32),
            pltpu.VMEM((4, levels, 8, cells), f32),
            pltpu.VMEM((rows, cells), i32),
            pltpu.VMEM((edge_rows, cells), f32),
            pltpu.VMEM((edge_rows, cells), f32),
            pltpu.SemaphoreType.DMA((3,)),
            pltpu.SemaphoreType.DMA((4,)),
            pltpu.SemaphoreType.DMA((4,)),
            pltpu.SemaphoreType.DMA((2,)),
        ],
        compiler_params=whole_grant,
        name="pack",
    )(
        sec, routes.reshape(block_count), dst_block.reshape(block_count),
        weight_index.reshape(block_count), atm_state, depth_levels, ocean_temp, vel_v,
    )

    north_to = [(tiles + t, tiles + t + 1) for t in range(tiles - 1)]
    south_to = [(t + 1, t) for t in range(tiles, 2 * tiles - 1)]
    south = lax.ppermute(up, ("sec", "tile"), north_to)
    north = lax.ppermute(down, ("sec", "tile"), south_to)
    payload, south, north = lax.optimization_barrier((payload, south, north))
    moved = lax.all_to_all(payload, "tile", split_axis=0, concat_axis=0, tiled=True)

    level = lambda count: pl.BlockSpec((1, count, rows, cells), lambda i: (0, 0, 0, 0))
    top = pl.pallas_call(
        functools.partial(surface_kernel, levels),
        grid=(1,),
        out_shape=jax.ShapeDtypeStruct((3, patches, 128), f32),
        in_specs=[
            SMEM,
            level(2),
            level(1),
            level(1),
            pl.BlockSpec((1, rows, cells), lambda i: (0, 0, 0)),
            pl.BlockSpec((edge_rows, cells), lambda i: (0, 0)),
            pl.BlockSpec((edge_rows, cells), lambda i: (0, 0)),
        ],
        out_specs=pl.BlockSpec((3, patches, 128), lambda i: (0, 0, 0)),
        compiler_params=ocean_grant,
        name="surface",
    )(sec, ocean_temp, vel_u, vel_v, depth_levels, south, north)
    top = lax.ppermute(top, "sec", [(1, 0)])

    steps = levels // LEVELS
    slab = pl.BlockSpec((1, LEVELS, rows, cells), lambda i, sec: (0, i * sec[0], 0, 0))
    fixed3 = pl.BlockSpec((1, rows, cells), lambda i, sec: (0, 0, 0))
    fixed2 = pl.BlockSpec((edge_rows, cells), lambda i, sec: (0, 0))
    out = pl.pallas_call(
        functools.partial(ocean_kernel, levels),
        grid_spec=pltpu.PrefetchScalarGridSpec(
            num_scalar_prefetch=1,
            grid=(steps,),
            in_specs=[
                slab,
                pl.BlockSpec(
                    (1, 1, rows, cells),
                    lambda i, sec: (0, jnp.minimum((i + 1) * LEVELS, levels - 1) * sec[0], 0, 0),
                ),
                slab,
                slab,
                fixed3,
                fixed2,
                fixed2,
            ],
            out_specs=pl.BlockSpec((1, LEVELS, rows, cells), lambda i, sec: (0, i, 0, 0)),
            scratch_shapes=[
                pltpu.VMEM((rows, cells), i32),
                pltpu.VMEM((rows, cells), i32),
                pltpu.VMEM((8, cells), i32),
                pltpu.VMEM((rows, cells), f32),
            ],
        ),
        out_shape=jax.ShapeDtypeStruct(ocean_temp.shape, f32),
        compiler_params=ocean_grant,
        cost_estimate=pl.CostEstimate(
            flops=40 * levels * rows * cells,
            bytes_accessed=17 * levels * rows * cells,
            transcendentals=0,
        ),
        name="ocean",
    )(sec, ocean_temp, ocean_temp, vel_u, vel_v, depth_levels, south, north)

    moved, out = lax.optimization_barrier((moved, out))
    ret, fresh = pl.pallas_call(
        functools.partial(heat_kernel, tiles),
        out_shape=(
            jax.ShapeDtypeStruct((slots, 128), f32),
            jax.ShapeDtypeStruct((patches, 128), f32),
        ),
        in_specs=[SMEM, VMEM, VMEM, VMEM],
        out_specs=(VMEM, VMEM),
        scratch_shapes=[pltpu.VMEM((slots, 128), bf16), pltpu.VMEM((slots, 768), bf16)],
        compiler_params=grant,
        name="heat",
    )(sec, moved, top, area_table)

    fresh = lax.ppermute(fresh, "sec", [(0, 1)])
    back = lax.all_to_all(ret, "tile", split_axis=0, concat_axis=0, tiled=True)
    following = pl.pallas_call(
        settle_kernel,
        grid=(1,),
        out_shape=jax.ShapeDtypeStruct(out.shape, f32),
        in_specs=[pl.BlockSpec((patches, 128), lambda i: (0, 0)), ANY],
        out_specs=level(1),
        input_output_aliases={1: 0},
        name="settle",
    )(fresh, out)
    skin = back.at[slot_of].get(mode="promise_in_bounds")
    return following, skin[None]


def solution(mesh):
    return jax.shard_map(
        body,
        mesh=mesh,
        in_specs=(
            P("sec", "tile", None, None),
            P("sec", "tile", None),
            P("sec", "tile"),
            P("sec", "tile"),
            P(),
            P("sec", None, "tile", None),
            P("sec", None, "tile", None),
            P("sec", None, "tile", None),
            P("sec", "tile", None),
        ),
        out_specs=(P("sec", None, "tile", None), P("sec", "tile", None)),
        check_vma=False,
    )
```

time: 106 us -> 86.3 us (0.81)
  the two profiles are of different devices: /device:TPU:0 before, /device:TPU:1 now
where the time goes in v2:
time: 86.3 us; the launch traced here: 85.6 us
  starting transfers between devices  37.8 us (44%)
  Pallas kernels  25.8 us (30%)
  waiting for transfers between devices  18.9 us (22%)
  local copies, waits for them, and re-layouts  2.28 us (3%)
    all_to_all x1, starting transfers between devices, body(): lax.all_to_all(payload, 'tile', split_axis=0, concat_axis=0, tiled=True)  20.6 us
    pallas_call x1, Pallas kernels, body(): pl.pallas_call(functools.partial(ocean_kernel, levels), grid_spec=pltpu.P...  15.2 us
    all_to_all x1, starting transfers between devices, body(): back = lax.all_to_all(ret, 'tile', split_axis=0, concat_axis=0, tiled=True)  8.8 us
    ppermute x1, waiting for transfers between devices, body(): south = lax.ppermute(up, ('sec', 'tile'), north_to)  6.84 us
    pallas_call x1, Pallas kernels, body(): pl.pallas_call(functools.partial(pack_kernel, tiles), out_shape=(jax.Shap...  5.88 us
    all_to_all x1, waiting for transfers between devices, body(): back = lax.all_to_all(ret, 'tile', split_axis=0, concat_axis=0, tiled=True)  5.27 us
    ppermute x1, starting transfers between devices, body(): south = lax.ppermute(up, ('sec', 'tile'), north_to)  4.41 us
    ppermute x1, waiting for transfers between devices, body(): north = lax.ppermute(down, ('sec', 'tile'), south_to)  4 us
  transfers between devices with their start and end apart: 6, of which 5 were waited for; matrix products, arithmetic and copies ran while one was open for 0% of the time, Pallas kernels for 22%

profile of v2, /device:TPU:1, one launch (start us, length us, event | category | flops | bytes accessed | tf_op | source)
XLA Modules:
  0.0 85.6 jit_solution(14595669618931746311)
XLA Ops:
  0.6 5.9 %pack.1 = (f32[1152,4,128]{2,1,0:T(4,128)}, s32[512]{0:T(512)}, f32[168,1024]{1,0:T(8,128)}, f32[168,1024]{1,0:T(8,128)}) custom-call(s32[1]{0:T(128)} %bitcast.sec, s32[512]{0:T(512)} %bitcast.9, s32[512]{0:T(512)} %bitcast.10, s32[512]{0:T(512)} %bitcast.11, f32[1,512,4,128]{3,2,1,0:T(4,128)} %state_in.1, s32[1,16,1024]{2,1,0:T(8,128)} %depth.3, ...), custom_call_target="tpu_custom_call" | custom-call | tf_op jit(solution)/shard_map/pack/pallas_call | solution.py:348
  6.5 4.4 %collective-permute-start = (f32[168,1024]{1,0:T(8,128)}, f32[168,1024]{1,0:T(8,128)S(1)}, u32[]{:S(2)}, u32[]{:S(2)}) collective-permute-start(f32[168,1024]{1,0:T(8,128)} %get-tuple-element.14), channel_id=1, source_target_pairs={{64,65},{65,66},{66,67},{67,68},{68,69},{69,70},{70,71},{71,72},{7... | collective-permute-start | bytes 2064392 | tf_op jit(solution)/shard_map/ppermute | solution.py:384
  10.9 1.3 %collective-permute-start.1 = (f32[168,1024]{1,0:T(8,128)}, f32[168,1024]{1,0:T(8,128)}, u32[]{:S(2)}, u32[]{:S(2)}) collective-permute-start(f32[168,1024]{1,0:T(8,128)} %get-tuple-element.15), channel_id=1, source_target_pairs={{65,64},{66,65},{67,66},{68,67},{69,68},{70,69},{71,70},{72,71},{7... | collective-permute-start | bytes 2064392 | tf_op jit(solution)/shard_map/ppermute | solution.py:385
  12.2 6.8 %collective-permute-done.south = f32[168,1024]{1,0:T(8,128)S(1)} collective-permute-done((f32[168,1024]{1,0:T(8,128)}, f32[168,1024]{1,0:T(8,128)S(1)}, u32[]{:S(2)}, u32[]{:S(2)}) %collective-permute-start) | collective-permute-done | bytes 688160 | tf_op jit(solution)/shard_map/ppermute | solution.py:384
  19.1 0.0 copy-start.1
  19.1 4.0 %collective-permute-done.1.north = f32[168,1024]{1,0:T(8,128)} collective-permute-done((f32[168,1024]{1,0:T(8,128)}, f32[168,1024]{1,0:T(8,128)}, u32[]{:S(2)}, u32[]{:S(2)}) %collective-permute-start.1) | collective-permute-done | bytes 688160 | tf_op jit(solution)/shard_map/ppermute | solution.py:385
  23.1 20.6 %all-to-all-start = ((f32[1152,4,128]{2,1,0:T(4,128)}), f32[1152,4,128]{2,1,0:T(4,128)S(1)}, u32[]{:S(2)}, u32[]{:S(2)}) async-start(f32[1152,4,128]{2,1,0:T(4,128)} %get-tuple-element.16), calls=%async_computation | async-start | bytes 4718592 | tf_op jit(solution)/shard_map/all_to_all | solution.py:387
  43.7 0.0 copy-done.1
  43.7 2.4 %surface.1 = f32[3,128,128]{2,1,0:T(8,128)} custom-call(s32[1]{0:T(128)} %bitcast.sec, f32[1,80,16,1024]{3,2,1,0:T(8,128)} %temp.5, f32[1,80,16,1024]{3,2,1,0:T(8,128)} %zonal.3, f32[1,80,16,1024]{3,2,1,0:T(8,128)} %merid.5, s32[1,16,1024]{2,1,0:T(8,128)} %depth.3, f32[168,1024]{1,0:T(8,128)} %copy-done.1, f32[168,1024]{1,0:T(8,128)} %collective-permute-done.1.north), custom_call_target="tpu_custom_call" | custom-call | tf_op jit(solution)/shard_map/surface/pallas_call | solution.py:390
  46.1 0.0 copy-start
  46.1 0.0 copy-start.3
  46.1 1.4 %collective-permute-start.2 = (f32[3,128,128]{2,1,0:T(8,128)}, f32[3,128,128]{2,1,0:T(8,128)S(1)}, u32[]{:S(2)}, u32[]{:S(2)}) collective-permute-start(f32[3,128,128]{2,1,0:T(8,128)} %surface.1), channel_id=1, source_target_pairs={{64,0},{65,1},{66,2},{67,3},{68,4},{69,5},{70,6},{71,7},{72,8},{73... | collective-permute-start | bytes 589832 | tf_op jit(solution)/shard_map/ppermute | solution.py:407
  47.5 15.2 %ocean.1.whole = f32[1,80,16,1024]{3,2,1,0:T(8,128)} custom-call(s32[1]{0:T(128)} %bitcast.sec, f32[1,80,16,1024]{3,2,1,0:T(8,128)} %temp.5, f32[1,80,16,1024]{3,2,1,0:T(8,128)} %temp.5, f32[1,80,16,1024]{3,2,1,0:T(8,128)} %zonal.3, f32[1,80,16,1024]{3,2,1,0:T(8,128)} %merid.5, s32[1,16,1024]{2,1,0:T(8,128)} %depth.3, f32[168,1024]{1,0:T(8,128)} %copy-done.1, ...), custom_call_target="tpu_custom_call" | custom-call | flops 52428800 | bytes 22282240 | tf_op jit(solution)/shard_map/ocean/pallas_call | solution.py:413
  62.7 1.0 %all-to-all-done.payload = f32[1152,4,128]{2,1,0:T(4,128)S(1)} async-done(((f32[1152,4,128]{2,1,0:T(4,128)}), f32[1152,4,128]{2,1,0:T(4,128)S(1)}, u32[]{:S(2)}, u32[]{:S(2)}) %all-to-all-start) | async-done | bytes 2359328 | tf_op jit(solution)/shard_map/all_to_all | solution.py:387
  63.7 0.0 collective-permute-done.2.top
  63.7 0.0 copy-done
  63.7 0.8 heat.1
  64.6 8.8 %all-to-all-start.1 = ((f32[64,16,128]{2,1,0:T(8,128)}), f32[64,16,128]{2,1,0:T(8,128)S(1)}, u32[]{:S(2)}, u32[]{:S(2)}) async-start(f32[64,16,128]{2,1,0:T(8,128)} %bitcast.4), calls=%async_computation.1 | async-start | bytes 1048576 | tf_op jit(solution)/shard_map/all_to_all | solution.py:463
  73.4 0.0 copy-done.3
  73.4 1.3 %collective-permute-start.3 = (f32[128,128]{1,0:T(8,128)S(1)}, f32[128,128]{1,0:T(8,128)S(1)}, u32[]{:S(2)}, u32[]{:S(2)}) collective-permute-start(f32[128,128]{1,0:T(8,128)S(1)} %get-tuple-element.20), channel_id=1, source_target_pairs={{0,64},{1,65},{2,66},{3,67},{4,68},{5,69},{6,70},{7,71},{8,72},{9,... | collective-permute-start | bytes 196616 | tf_op jit(solution)/shard_map/ppermute | solution.py:462
  74.7 1.8 %collective-permute-done.3.fresh = f32[128,128]{1,0:T(8,128)S(1)} collective-permute-done((f32[128,128]{1,0:T(8,128)S(1)}, f32[128,128]{1,0:T(8,128)S(1)}, u32[]{:S(2)}, u32[]{:S(2)}) %collective-permute-start.3) | collective-permute-done | bytes 65568 | tf_op jit(solution)/shard_map/ppermute | solution.py:462
  76.5 0.0 copy-start.2
  76.5 0.6 copy-done.2
  77.2 1.5 %settle.1 = f32[1,80,16,1024]{3,2,1,0:T(8,128)} custom-call(f32[128,128]{1,0:T(8,128)} %copy-done.2, f32[1,80,16,1024]{3,2,1,0:T(8,128)} %ocean.1.whole), custom_call_target="tpu_custom_call", output_to_operand_aliasing={{}: (1, {})} | custom-call | tf_op jit(solution)/shard_map/settle/pallas_call | solution.py:464
  78.7 5.3 %all-to-all-done.1 = f32[64,16,128]{2,1,0:T(8,128)S(1)} async-done(((f32[64,16,128]{2,1,0:T(8,128)}), f32[64,16,128]{2,1,0:T(8,128)S(1)}, u32[]{:S(2)}, u32[]{:S(2)}) %all-to-all-start.1) | async-done | bytes 524320 | tf_op jit(solution)/shard_map/all_to_all | solution.py:463
  83.9 1.6 %gather_fusion = f32[512,128]{1,0:T(8,128)} fusion(f32[1024,128]{1,0:T(8,128)S(1)} %bitcast.7, s32[1024]{0:T(1024)S(1)} %pad_clamp_fusion), kind=kCustom, calls=%fused_computation | custom fusion | bytes 526336 | tf_op jit(solution)/shard_map/gather | solution.py:473
  (2 shorter events, 0.0 us)
Async XLA Ops:
  6.5 12.6 %collective-permute-start = (f32[168,1024]{1,0:T(8,128)}, f32[168,1024]{1,0:T(8,128)S(1)}, u32[]{:S(2)}, u32[]{:S(2)}) collective-permute-start(f32[168,1024]{1,0:T(8,128)} %get-tuple-element.14), channel_id=1, source_target_pairs={{64,65},{65,66},{66,67},{67,68},{68,69},{69,70},{70,71},{71,72},{7... | collective-permute-start | bytes 2064392 | tf_op jit(solution)/shard_map/ppermute | solution.py:384
  10.9 12.1 %collective-permute-start.1 = (f32[168,1024]{1,0:T(8,128)}, f32[168,1024]{1,0:T(8,128)}, u32[]{:S(2)}, u32[]{:S(2)}) collective-permute-start(f32[168,1024]{1,0:T(8,128)} %get-tuple-element.15), channel_id=1, source_target_pairs={{65,64},{66,65},{67,66},{68,67},{69,68},{70,69},{71,70},{72,71},{7... | collective-permute-start | bytes 2064392 | tf_op jit(solution)/shard_map/ppermute | solution.py:385
  19.1 24.6 %copy-start.1 = (f32[168,1024]{1,0:T(8,128)}, f32[168,1024]{1,0:T(8,128)S(1)}, u32[]{:S(2)}) copy-start(f32[168,1024]{1,0:T(8,128)S(1)} %collective-permute-done.south) | copy-start | bytes 2064388
  23.1 40.6 %all-to-all-start = ((f32[1152,4,128]{2,1,0:T(4,128)}), f32[1152,4,128]{2,1,0:T(4,128)S(1)}, u32[]{:S(2)}, u32[]{:S(2)}) async-start(f32[1152,4,128]{2,1,0:T(4,128)} %get-tuple-element.16), calls=%async_computation | async-start | bytes 4718592 | tf_op jit(solution)/shard_map/all_to_all | solution.py:387
  46.1 17.6 %copy-start = (f32[16,128]{1,0:T(8,128)S(1)}, f32[16,128]{1,0:T(8,128)}, u32[]{:S(2)}) copy-start(f32[16,128]{1,0:T(8,128)} %table.1) | copy-start | bytes 24580
  46.1 27.3 %copy-start.3 = (s32[512]{0:T(512)S(1)}, s32[512]{0:T(512)}, u32[]{:S(2)}) copy-start(s32[512]{0:T(512)} %get-tuple-element.23) | copy-start | bytes 6148
  46.1 17.6 %collective-permute-start.2 = (f32[3,128,128]{2,1,0:T(8,128)}, f32[3,128,128]{2,1,0:T(8,128)S(1)}, u32[]{:S(2)}, u32[]{:S(2)}) collective-permute-start(f32[3,128,128]{2,1,0:T(8,128)} %surface.1), channel_id=1, source_target_pairs={{64,0},{65,1},{66,2},{67,3},{68,4},{69,5},{70,6},{71,7},{72,8},{73... | collective-permute-start | bytes 589832 | tf_op jit(solution)/shard_map/ppermute | solution.py:407
  64.6 19.4 %all-to-all-start.1 = ((f32[64,16,128]{2,1,0:T(8,128)}), f32[64,16,128]{2,1,0:T(8,128)S(1)}, u32[]{:S(2)}, u32[]{:S(2)}) async-start(f32[64,16,128]{2,1,0:T(8,128)} %bitcast.4), calls=%async_computation.1 | async-start | bytes 1048576 | tf_op jit(solution)/shard_map/all_to_all | solution.py:463
  73.4 3.1 %collective-permute-start.3 = (f32[128,128]{1,0:T(8,128)S(1)}, f32[128,128]{1,0:T(8,128)S(1)}, u32[]{:S(2)}, u32[]{:S(2)}) collective-permute-start(f32[128,128]{1,0:T(8,128)S(1)} %get-tuple-element.20), channel_id=1, source_target_pairs={{0,64},{1,65},{2,66},{3,67},{4,68},{5,69},{6,70},{7,71},{8,72},{9,... | collective-permute-start | bytes 196616 | tf_op jit(solution)/shard_map/ppermute | solution.py:462
  76.5 0.6 copy-start.2

commit v3 on v2

--- a/solution.py
+++ b/solution.py
@@ -28,9 +28,9 @@
 
 def pack_kernel(
     tiles, sec, dest_in, block_in, row_in, state_in, depth_in, temp, merid,
-    payload_out, slot_of, up_out, down_out,
+    payload_out, slot_of, up_out, down_out, blank,
     dest, block, row, state, payload, count, entry, edge, depth, up, down,
-    index_sem, state_sem, edge_sem, out_sem,
+    nothing, index_sem, state_sem, edge_sem, out_sem, blank_sem,
 ):
     levels = temp.shape[1]
     rows = temp.shape[2]
@@ -55,6 +55,15 @@
             for n in range(pieces)
         ]
         for copy in indices + states:
+            copy.start()
+        nothing[...] = jnp.zeros_like(nothing)
+        blanks = [
+            pltpu.make_async_copy(
+                nothing, blank.at[0, pl.ds(n * LEVELS, LEVELS)], blank_sem.at[n]
+            )
+            for n in range(levels // LEVELS)
+        ]
+        for copy in blanks:
             copy.start()
 
         for i in range(tiles):
@@ -102,13 +111,13 @@
         ]
         for copy in outs:
             copy.start()
-        for copy in outs:
+        for copy in outs + blanks:
             copy.wait()
 
     @pl.when(sec[0] != 0)
     def _():
-        bring = pltpu.make_async_copy(depth_in.at[0], depth, index_sem.at[0])
-        bring.start()
+        depth_copy = pltpu.make_async_copy(depth_in.at[0], depth, index_sem.at[0])
+        depth_copy.start()
         copies = [
             pltpu.make_async_copy(field.at[0, :, pl.ds(lo, 8), :], edge.at[n], edge_sem.at[n])
             for n, (field, lo) in enumerate(
@@ -124,7 +133,7 @@
             return 0
 
         lax.fori_loop(0, blocks // UNROLL, none, 0)
-        bring.wait()
+        depth_copy.wait()
         cells = depth.shape[1]
         up[2 * levels :, :] = jnp.broadcast_to(depth[rows - 1 :, :].astype(f32), (8, cells))
         down[2 * levels :, :] = jnp.broadcast_to(depth[0:1, :].astype(f32), (8, cells))
@@ -142,7 +151,7 @@
             copy.wait()
 
 
-def faces(levels, k, t, u, v, north, south, depth_e, depth_n, depth_s):
+def faces(k, t, u, v, t_north, v_north, t_s, v_s, depth_e, depth_n, depth_s):
     rows, cells = t.shape
     first = iota((rows, cells), 0) == 0
     last = iota((rows, cells), 0) == rows - 1
@@ -153,15 +162,13 @@
         HEAT_DIFFUSION * (t_e - t) - (0.25 * (u + u_e)) * (t + t_e),
         0.0,
     )
-    t_n = jnp.where(last, north[pl.ds(k, 1), :], pltpu.roll(t, rows - 1, 0))
-    v_n = jnp.where(last, north[pl.ds(levels + k, 1), :], pltpu.roll(v, rows - 1, 0))
+    t_n = jnp.where(last, t_north, pltpu.roll(t, rows - 1, 0))
+    v_n = jnp.where(last, v_north, pltpu.roll(v, rows - 1, 0))
     northward = jnp.where(
         k < depth_n,
         HEAT_DIFFUSION * (t_n - t) - (0.25 * (v + v_n)) * (t + t_n),
         0.0,
     )
-    t_s = south[pl.ds(k, 1), :]
-    v_s = south[pl.ds(levels + k, 1), :]
     t_0 = t[0:1]
     southmost = jnp.where(
         k < depth_s,
@@ -173,11 +180,10 @@
     )
 
 
-def face_depths(levels, d, north, south):
+def face_depths(d, d_north, d_south):
     rows, cells = d.shape
     last = iota((rows, cells), 0) == rows - 1
-    d_north = north[2 * levels : 2 * levels + 1, :].astype(i32)
-    d_south = south[2 * levels : 2 * levels + 1, :].astype(i32)
+    d_north, d_south = d_north.astype(i32), d_south.astype(i32)
     return (
         jnp.minimum(d, pltpu.roll(d, cells - 1, 1)),
         jnp.minimum(d, jnp.where(last, d_north, pltpu.roll(d, rows - 1, 0))),
@@ -185,63 +191,101 @@
     )
 
 
-def surface_kernel(levels, sec, temp, zonal, merid, depth, south, north, top):
+def bring(copies):
+    for copy in copies:
+        copy.start()
+    for copy in copies:
+        copy.wait()
+
+
+def surface_kernel(
+    levels, sec, temp, zonal, merid, depth, south, north,
+    top,
+    t_in, u_in, v_in, d_in, edge, made, sem, out_sem,
+):
     @pl.when(sec[0] != 0)
     def _():
-        d = depth[0]
+        pairs = [
+            (temp.at[0, 0:2], t_in),
+            (zonal.at[0, 0], u_in),
+            (merid.at[0, 0], v_in),
+            (depth.at[0], d_in),
+        ] + [
+            (side.at[pl.ds(n * levels, 8)], edge.at[3 * m + n])
+            for m, side in enumerate((north, south))
+            for n in range(3)
+        ]
+        bring([pltpu.make_async_copy(*pair, sem.at[n]) for n, pair in enumerate(pairs)])
+        d = d_in[...]
         rows, cells = d.shape
-        t = temp[0, 0]
-        below = jnp.where(1 < d, VERTICAL_MIXING * (temp[0, 1] - t), 0.0)
+        t = t_in[0]
+        row = [edge[n, 0:1, :] for n in range(6)]
+        below = jnp.where(1 < d, VERTICAL_MIXING * (t_in[1] - t), 0.0)
         base = t + faces(
-            levels, 0, t, zonal[0, 0], merid[0, 0], north, south,
-            *face_depths(levels, d, north, south),
+            0, t, u_in[...], v_in[...], row[0], row[1], row[3], row[4],
+            *face_depths(d, row[2], row[5]),
         ) + below
         wet = jnp.where(d > 0, FLUX_GAIN, 0.0)
         patches = cells // 128
         for p in range(patches):
             part = slice(p * 128, p * 128 + 128)
-            top[0, pl.ds(p, rows, stride=patches), :] = t[:, part]
-            top[1, pl.ds(p, rows, stride=patches), :] = base[:, part]
-            top[2, pl.ds(p, rows, stride=patches), :] = wet[:, part]
+            made[0, pl.ds(p, rows, stride=patches), :] = t[:, part]
+            made[1, pl.ds(p, rows, stride=patches), :] = base[:, part]
+            made[2, pl.ds(p, rows, stride=patches), :] = wet[:, part]
+        bring([pltpu.make_async_copy(made, top, out_sem)])
 
 
 def ocean_kernel(
-    levels, sec, temp, beneath, zonal, merid, depth, south, north,
+    levels, sec, temp, zonal, merid, depth_in, south_in, north_in, blank,
     out,
-    depth_e, depth_n, depth_s, carry,
+    depth, south, north, depth_e, depth_n, depth_s, carry, sem,
 ):
-    step = pl.program_id(0)
-
-    @pl.when(sec[0] == 0)
-    def _():
-        out[...] = jnp.zeros_like(out)
+    rows, cells = depth.shape
 
     @pl.when(sec[0] != 0)
     def _():
-        @pl.when(step == 0)
-        def _():
-            e, n, s = face_depths(levels, depth[0], north, south)
-            depth_e[...] = e
-            depth_n[...] = n
-            depth_s[...] = jnp.broadcast_to(s, depth_s.shape)
-            carry[...] = jnp.zeros_like(carry)
-
-        above = carry[...]
-        for j in range(LEVELS):
-            k = step * LEVELS + j
-            t = temp[0, j]
-            under = beneath[0, 0] if j == LEVELS - 1 else temp[0, j + 1]
-            below = jnp.where(k + 1 < depth[0], VERTICAL_MIXING * (under - t), 0.0)
-            out[0, j] = (
-                t
-                + faces(
-                    levels, k, t, zonal[0, j], merid[0, j], north, south,
-                    depth_e[...], depth_n[...], depth_s[0:1, :],
+        pairs = [(depth_in.at[0], depth), (south_in, south), (north_in, north)]
+        bring([pltpu.make_async_copy(*pair, sem.at[n]) for n, pair in enumerate(pairs)])
+        e, n, s = face_depths(
+            depth[...], north[2 * levels : 2 * levels + 1, :], south[2 * levels : 2 * levels + 1, :]
+        )
+        depth_e[...] = e
+        depth_n[...] = n
+        depth_s[...] = jnp.broadcast_to(s, depth_s.shape)
+        carry[...] = jnp.zeros_like(carry)
+
+        def step(index, temp_in, beneath, zonal_in, merid_in, fresh):
+            i = index.index[0]
+            above = carry[...]
+            for j in range(LEVELS):
+                k = i * LEVELS + j
+                t = temp_in[0, j]
+                under = beneath[0, 0] if j == LEVELS - 1 else temp_in[0, j + 1]
+                below = jnp.where(k + 1 < depth[...], VERTICAL_MIXING * (under - t), 0.0)
+                fresh[0, j] = (
+                    t
+                    + faces(
+                        k, t, zonal_in[0, j], merid_in[0, j],
+                        north[pl.ds(k, 1), :], north[pl.ds(levels + k, 1), :],
+                        south[pl.ds(k, 1), :], south[pl.ds(levels + k, 1), :],
+                        depth_e[...], depth_n[...], depth_s[0:1, :],
+                    )
+                    + (below - above)
                 )
-                + (below - above)
-            )
-            above = below
-        carry[...] = above
+                above = below
+            carry[...] = above
+
+        slab = pl.BlockSpec((1, LEVELS, rows, cells), lambda i: (0, i, 0, 0))
+        next_level = pl.BlockSpec(
+            (1, 1, rows, cells), lambda i: (0, jnp.minimum((i + 1) * LEVELS, levels - 1), 0, 0)
+        )
+        pltpu.emit_pipeline(
+            step,
+            grid=(levels // LEVELS,),
+            in_specs=[slab, next_level, slab, slab],
+            out_specs=[slab],
+            _explicit_indices=True,
+        )(temp, temp, zonal, merid, out)
 
 
 def in_three(x):
@@ -324,11 +368,14 @@
         ret[...] = joined(jnp.dot(hit[...], in_three(new_top), preferred_element_type=f32))
 
 
-def settle_kernel(fresh, whole, out):
-    rows, cells = out.shape[2:]
-    patches = cells // 128
-    for p in range(patches):
-        out[0, 0, :, p * 128 : p * 128 + 128] = fresh[pl.ds(p, rows, stride=patches), :]
+def settle_kernel(sec, fresh, whole, out, level, sem):
+    @pl.when(sec[0] != 0)
+    def _():
+        rows, cells = level.shape
+        patches = cells // 128
+        for p in range(patches):
+            level[:, p * 128 : p * 128 + 128] = fresh[pl.ds(p, rows, stride=patches), :]
+        bring([pltpu.make_async_copy(level, out.at[0, 0], sem)])
 
 
 def body(
@@ -345,16 +392,17 @@
     whole_grant = pltpu.CompilerParams(vmem_limit_bytes=60 << 20)
 
     edge_rows = 2 * levels + 8
-    payload, slot_of, up, down = pl.pallas_call(
+    payload, slot_of, up, down, blank = pl.pallas_call(
         functools.partial(pack_kernel, tiles),
         out_shape=(
             jax.ShapeDtypeStruct((tiles * CHUNK, 4, 128), f32),
             jax.ShapeDtypeStruct((block_count,), i32),
             jax.ShapeDtypeStruct((edge_rows, cells), f32),
             jax.ShapeDtypeStruct((edge_rows, cells), f32),
+            jax.ShapeDtypeStruct(ocean_temp.shape, f32),
         ),
         in_specs=[SMEM] + [HBM] * 7,
-        out_specs=(HBM, SMEM, HBM, HBM),
+        out_specs=(HBM, SMEM, HBM, HBM, HBM),
         scratch_shapes=[
             pltpu.SMEM((block_count,), i32),
             pltpu.SMEM((block_count,), i32),
@@ -367,10 +415,12 @@
             pltpu.VMEM((rows, cells), i32),
             pltpu.VMEM((edge_rows, cells), f32),
             pltpu.VMEM((edge_rows, cells), f32),
+            pltpu.VMEM((LEVELS, rows, cells), f32),
             pltpu.SemaphoreType.DMA((3,)),
             pltpu.SemaphoreType.DMA((4,)),
             pltpu.SemaphoreType.DMA((4,)),
             pltpu.SemaphoreType.DMA((2,)),
+            pltpu.SemaphoreType.DMA((levels // LEVELS,)),
         ],
         compiler_params=whole_grant,
         name="pack",
@@ -379,63 +429,57 @@
         weight_index.reshape(block_count), atm_state, depth_levels, ocean_temp, vel_v,
     )
 
+    def among_atmosphere(value):
+        return lax.cond(
+            sec[0] == 0,
+            lambda v: lax.all_to_all(v, "tile", split_axis=0, concat_axis=0, tiled=True),
+            lambda v: v,
+            value,
+        )
+
     north_to = [(tiles + t, tiles + t + 1) for t in range(tiles - 1)]
     south_to = [(t + 1, t) for t in range(tiles, 2 * tiles - 1)]
     south = lax.ppermute(up, ("sec", "tile"), north_to)
     north = lax.ppermute(down, ("sec", "tile"), south_to)
-    payload, south, north = lax.optimization_barrier((payload, south, north))
-    moved = lax.all_to_all(payload, "tile", split_axis=0, concat_axis=0, tiled=True)
-
-    level = lambda count: pl.BlockSpec((1, count, rows, cells), lambda i: (0, 0, 0, 0))
     top = pl.pallas_call(
         functools.partial(surface_kernel, levels),
-        grid=(1,),
         out_shape=jax.ShapeDtypeStruct((3, patches, 128), f32),
-        in_specs=[
-            SMEM,
-            level(2),
-            level(1),
-            level(1),
-            pl.BlockSpec((1, rows, cells), lambda i: (0, 0, 0)),
-            pl.BlockSpec((edge_rows, cells), lambda i: (0, 0)),
-            pl.BlockSpec((edge_rows, cells), lambda i: (0, 0)),
+        in_specs=[SMEM] + [HBM] * 6,
+        out_specs=HBM,
+        scratch_shapes=[
+            pltpu.VMEM((2, rows, cells), f32),
+            pltpu.VMEM((rows, cells), f32),
+            pltpu.VMEM((rows, cells), f32),
+            pltpu.VMEM((rows, cells), i32),
+            pltpu.VMEM((6, 8, cells), f32),
+            pltpu.VMEM((3, patches, 128), f32),
+            pltpu.SemaphoreType.DMA((10,)),
+            pltpu.SemaphoreType.DMA(()),
         ],
-        out_specs=pl.BlockSpec((3, patches, 128), lambda i: (0, 0, 0)),
         compiler_params=ocean_grant,
         name="surface",
     )(sec, ocean_temp, vel_u, vel_v, depth_levels, south, north)
+    payload, top = lax.optimization_barrier((payload, top))
     top = lax.ppermute(top, "sec", [(1, 0)])
-
-    steps = levels // LEVELS
-    slab = pl.BlockSpec((1, LEVELS, rows, cells), lambda i, sec: (0, i * sec[0], 0, 0))
-    fixed3 = pl.BlockSpec((1, rows, cells), lambda i, sec: (0, 0, 0))
-    fixed2 = pl.BlockSpec((edge_rows, cells), lambda i, sec: (0, 0))
+    moved = among_atmosphere(payload)
+
+    moved, south, north = lax.optimization_barrier((moved, south, north))
     out = pl.pallas_call(
         functools.partial(ocean_kernel, levels),
-        grid_spec=pltpu.PrefetchScalarGridSpec(
-            num_scalar_prefetch=1,
-            grid=(steps,),
-            in_specs=[
-                slab,
-                pl.BlockSpec(
-                    (1, 1, rows, cells),
-                    lambda i, sec: (0, jnp.minimum((i + 1) * LEVELS, levels - 1) * sec[0], 0, 0),
-                ),
-                slab,
-                slab,
-                fixed3,
-                fixed2,
-                fixed2,
-            ],
-            out_specs=pl.BlockSpec((1, LEVELS, rows, cells), lambda i, sec: (0, i, 0, 0)),
-            scratch_shapes=[
-                pltpu.VMEM((rows, cells), i32),
-                pltpu.VMEM((rows, cells), i32),
-                pltpu.VMEM((8, cells), i32),
-                pltpu.VMEM((rows, cells), f32),
-            ],
-        ),
+        in_specs=[SMEM] + [HBM] * 7,
+        out_specs=HBM,
         out_shape=jax.ShapeDtypeStruct(ocean_temp.shape, f32),
+        scratch_shapes=[
+            pltpu.VMEM((rows, cells), i32),
+            pltpu.VMEM((edge_rows, cells), f32),
+            pltpu.VMEM((edge_rows, cells), f32),
+            pltpu.VMEM((rows, cells), i32),
+            pltpu.VMEM((rows, cells), i32),
+            pltpu.VMEM((8, cells), i32),
+            pltpu.VMEM((rows, cells), f32),
+            pltpu.SemaphoreType.DMA((3,)),
+        ],
+        input_output_aliases={7: 0},
         compiler_params=ocean_grant,
         cost_estimate=pl.CostEstimate(
             flops=40 * levels * rows * cells,
@@ -443,9 +487,8 @@
             transcendentals=0,
         ),
         name="ocean",
-    )(sec, ocean_temp, ocean_temp, vel_u, vel_v, depth_levels, south, north)
-
-    moved, out = lax.optimization_barrier((moved, out))
+    )(sec, ocean_temp, vel_u, vel_v, depth_levels, south, north, blank)
+
     ret, fresh = pl.pallas_call(
         functools.partial(heat_kernel, tiles),
         out_shape=(
@@ -460,16 +503,16 @@
     )(sec, moved, top, area_table)
 
     fresh = lax.ppermute(fresh, "sec", [(0, 1)])
-    back = lax.all_to_all(ret, "tile", split_axis=0, concat_axis=0, tiled=True)
+    back = among_atmosphere(ret)
     following = pl.pallas_call(
         settle_kernel,
-        grid=(1,),
         out_shape=jax.ShapeDtypeStruct(out.shape, f32),
-        in_specs=[pl.BlockSpec((patches, 128), lambda i: (0, 0)), ANY],
-        out_specs=level(1),
-        input_output_aliases={1: 0},
+        in_specs=[SMEM, VMEM, HBM],
+        out_specs=HBM,
+        scratch_shapes=[pltpu.VMEM((rows, cells), f32), pltpu.SemaphoreType.DMA(())],
+        input_output_aliases={2: 0},
         name="settle",
-    )(fresh, out)
+    )(sec, fresh, out)
     skin = back.at[slot_of].get(mode="promise_in_bounds")
     return following, skin[None]
 

time: 86.3 us -> 69.4 us (0.80)
  the two profiles are of different devices: /device:TPU:1 before, /device:TPU:0 now
where the time goes in v3:
time: 69.4 us; the launch traced here: 68.9 us
  blocking collectives  49.7 us (72%)
  Pallas kernels  10.2 us (15%)
  starting transfers between devices  4.84 us (7%)
  local copies, waits for them, and re-layouts  3.35 us (5%)
  between operations  0.73 us (1%)
    all_to_all x2, blocking collectives, among_atmosphere(): lax.all_to_all(v, 'tile', split_axis=0, concat_axis=0, tiled=True)  49.7 us
    pallas_call x1, Pallas kernels, body(): pl.pallas_call(functools.partial(pack_kernel, tiles), out_shape=(jax.Shap...  5.34 us
    pallas_call x1, Pallas kernels, body(): pl.pallas_call(functools.partial(heat_kernel, tiles), out_shape=(jax.Shap...  3.83 us
    gather x1, local copies, waits for them, and re-layouts, body(): skin = back.at[slot_of].get(mode='promise_in_bounds')  1.64 us
    ppermute x1, starting transfers between devices, body(): north = lax.ppermute(down, ('sec', 'tile'), south_to)  1.55 us
    unnamed x8, local copies, waits for them, and re-layouts  1.47 us
  transfers between devices with their start and end apart: 4, of which 0 were waited for; matrix products, arithmetic and copies ran while one was open for 3% of the time, Pallas kernels for 0%

profile of v3, /device:TPU:0, one launch (start us, length us, event | category | flops | bytes accessed | tf_op | source)
XLA Modules:
  0.0 68.9 jit_solution(511991048542125769)
XLA Ops:
  0.6 5.3 %pack.1 = (f32[1152,4,128]{2,1,0:T(4,128)S(1)}, s32[512]{0:T(512)}, f32[168,1024]{1,0:T(8,128)}, f32[168,1024]{1,0:T(8,128)}, f32[1,80,16,1024]{3,2,1,0:T(8,128)}) custom-call(s32[1]{0:T(128)} %bitcast.2.sec, s32[512]{0:T(512)} %bitcast.10, s32[512]{0:T(512)} %bitcast.11, s32[512]{0:T(512)} %bitcast.12, f32[1,512,4,128]{3,2,1,0:T(4,128)} %state_in.1, ...), custom_call_target="tpu_custom_call" | custom-call | tf_op jit(solution)/shard_map/pack/pallas_call | solution.py:395
  6.0 0.7 %collective-permute-start = (f32[168,1024]{1,0:T(8,128)}, f32[168,1024]{1,0:T(8,128)S(1)}, u32[]{:S(2)}, u32[]{:S(2)}) collective-permute-start(f32[168,1024]{1,0:T(8,128)} %get-tuple-element.25), channel_id=1, source_target_pairs={{64,65},{65,66},{66,67},{67,68},{68,69},{69,70},{70,71},{71,72},{7... | collective-permute-start | bytes 2064392 | tf_op jit(solution)/shard_map/ppermute | solution.py:442
  6.7 1.5 %collective-permute-start.1 = (f32[168,1024]{1,0:T(8,128)}, f32[168,1024]{1,0:T(8,128)}, u32[]{:S(2)}, u32[]{:S(2)}) collective-permute-start(f32[168,1024]{1,0:T(8,128)} %get-tuple-element.26), channel_id=1, source_target_pairs={{65,64},{66,65},{67,66},{68,67},{69,68},{70,69},{71,70},{72,71},{7... | collective-permute-start | bytes 2064392 | tf_op jit(solution)/shard_map/ppermute | solution.py:443
  8.2 0.0 copy-start.3
  8.2 0.0 collective-permute-done.south.south_in
  8.2 0.0 copy-start.1
  8.3 0.0 collective-permute-done.1.north.north_in
  8.3 0.8 %copy-done.1 = f32[168,1024]{1,0:T(8,128)} copy-done((f32[168,1024]{1,0:T(8,128)}, f32[168,1024]{1,0:T(8,128)S(1)}, u32[]{:S(2)}) %copy-start.1) | copy-done | bytes 688152
  9.1 0.1 surface.1
  9.2 0.0 copy-start
  9.2 1.3 %collective-permute-start.2 = (f32[3,128,128]{2,1,0:T(8,128)}, f32[3,128,128]{2,1,0:T(8,128)S(1)}, u32[]{:S(2)}, u32[]{:S(2)}) collective-permute-start(f32[3,128,128]{2,1,0:T(8,128)} %surface.1), channel_id=1, source_target_pairs={{64,0},{65,1},{66,2},{67,3},{68,4},{69,5},{70,6},{71,7},{72,8},{73... | collective-permute-start | bytes 589832 | tf_op jit(solution)/shard_map/ppermute | solution.py:463
  10.5 0.0 copy-done.3
  10.5 33.2 %conditional.2 = (f32[1152,4,128]{2,1,0:T(4,128)S(1)}) conditional(s32[]{:T(128)} %convert_element_type.4, f32[1152,4,128]{2,1,0:T(4,128)S(1)} %get-tuple-element.27, f32[1152,4,128]{2,1,0:T(4,128)S(1)} %get-tuple-element.27), branch_computations={%region_0.0_spmd, %region_1.0_spmd} | conditional | bytes 9437192 | solution.py:433
  10.6 0.2 copy.19
  10.8 33.0 %all_to_all.13 = f32[1152,4,128]{2,1,0:T(4,128)S(1)} all-to-all(f32[1152,4,128]{2,1,0:T(4,128)S(1)} %copy.19), channel_id=1, replica_groups=mesh['sec'=2,'tile'=64] {'tile'}, dimensions={0} | all-to-all | bytes 4718592 | tf_op jit(solution)/shard_map/cond/branch_1_fun/all_to_all | solution.py:435
  43.7 0.0 collective-permute-done.2.top
  43.7 0.0 copy-done
  43.7 3.8 %heat.1 = (f32[1024,128]{1,0:T(8,128)S(1)}, f32[128,128]{1,0:T(8,128)S(1)}) custom-call(s32[1]{0:T(128)} %bitcast.2.sec, f32[1152,4,128]{2,1,0:T(4,128)S(1)} %get-tuple-element.36.payload, f32[3,128,128]{2,1,0:T(8,128)S(1)} %collective-permute-done.2.top, f32[16,128]{1,0:T(8,128)S(1)} %copy-done), custom_call_target="tpu_custom_call" | custom-call | tf_op jit(solution)/shard_map/heat/pallas_call | solution.py:492
  47.6 1.3 %collective-permute-start.3 = (f32[128,128]{1,0:T(8,128)S(1)}, f32[128,128]{1,0:T(8,128)S(1)}, u32[]{:S(2)}, u32[]{:S(2)}) collective-permute-start(f32[128,128]{1,0:T(8,128)S(1)} %get-tuple-element.30), channel_id=1, source_target_pairs={{0,64},{1,65},{2,66},{3,67},{4,68},{5,69},{6,70},{7,71},{8,72},{9,... | collective-permute-start | bytes 196616 | tf_op jit(solution)/shard_map/ppermute | solution.py:505
  48.9 16.8 %conditional.3 = (f32[1024,128]{1,0:T(8,128)S(1)}) conditional(s32[]{:T(128)} %convert_element_type.4, f32[1024,128]{1,0:T(8,128)S(1)} %get-tuple-element.34, f32[1024,128]{1,0:T(8,128)S(1)} %get-tuple-element.34), branch_computations={%region_2.0_spmd, %region_3.0_spmd} | conditional | bytes 2097160 | solution.py:433
  49.0 16.8 %all_to_all.14 = f32[64,16,128]{2,1,0:T(8,128)S(1)} all-to-all(f32[64,16,128]{2,1,0:T(8,128)S(1)} %copy.20), channel_id=1, replica_groups=mesh['sec'=2,'tile'=64] {'tile'}, dimensions={0} | all-to-all | bytes 1048576 | tf_op jit(solution)/shard_map/cond/branch_1_fun/all_to_all | solution.py:435
  65.8 1.6 %gather_fusion = f32[512,128]{1,0:T(8,128)} fusion(f32[1024,128]{1,0:T(8,128)S(1)} %get-tuple-element.37, s32[1024]{0:T(1024)S(1)} %pad_clamp_fusion), kind=kCustom, calls=%fused_computation | custom fusion | bytes 526336 | tf_op jit(solution)/shard_map/gather | solution.py:516
  67.4 0.0 collective-permute-done.3.fresh
  67.4 0.0 copy-start.2
  67.4 0.6 copy-done.2
  68.0 0.8 %settle.1 = f32[1,80,16,1024]{3,2,1,0:T(8,128)} custom-call(s32[1]{0:T(128)} %bitcast.2.sec, f32[128,128]{1,0:T(8,128)} %copy-done.2, f32[1,80,16,1024]{3,2,1,0:T(8,128)} %ocean.1.whole), custom_call_target="tpu_custom_call", output_to_operand_aliasing={{}: (2, {})} | custom-call | tf_op jit(solution)/shard_map/settle/pallas_call | solution.py:507
  (4 shorter events, 0.1 us)
Async XLA Ops:
  6.0 2.3 %collective-permute-start = (f32[168,1024]{1,0:T(8,128)}, f32[168,1024]{1,0:T(8,128)S(1)}, u32[]{:S(2)}, u32[]{:S(2)}) collective-permute-start(f32[168,1024]{1,0:T(8,128)} %get-tuple-element.25), channel_id=1, source_target_pairs={{64,65},{65,66},{66,67},{67,68},{68,69},{69,70},{70,71},{71,72},{7... | collective-permute-start | bytes 2064392 | tf_op jit(solution)/shard_map/ppermute | solution.py:442
  6.7 1.6 %collective-permute-start.1 = (f32[168,1024]{1,0:T(8,128)}, f32[168,1024]{1,0:T(8,128)}, u32[]{:S(2)}, u32[]{:S(2)}) collective-permute-start(f32[168,1024]{1,0:T(8,128)} %get-tuple-element.26), channel_id=1, source_target_pairs={{65,64},{66,65},{67,66},{68,67},{69,68},{70,69},{71,70},{72,71},{7... | collective-permute-start | bytes 2064392 | tf_op jit(solution)/shard_map/ppermute | solution.py:443
  8.2 2.3 %copy-start.3 = (s32[512]{0:T(512)S(1)}, s32[512]{0:T(512)}, u32[]{:S(2)}) copy-start(s32[512]{0:T(512)} %get-tuple-element.35) | copy-start | bytes 6148
  8.2 0.8 %copy-start.1 = (f32[168,1024]{1,0:T(8,128)}, f32[168,1024]{1,0:T(8,128)S(1)}, u32[]{:S(2)}) copy-start(f32[168,1024]{1,0:T(8,128)S(1)} %collective-permute-done.south.south_in) | copy-start | bytes 2064388
  9.2 34.5 %copy-start = (f32[16,128]{1,0:T(8,128)S(1)}, f32[16,128]{1,0:T(8,128)}, u32[]{:S(2)}) copy-start(f32[16,128]{1,0:T(8,128)} %table.1) | copy-start | bytes 24580
  9.2 34.5 %collective-permute-start.2 = (f32[3,128,128]{2,1,0:T(8,128)}, f32[3,128,128]{2,1,0:T(8,128)S(1)}, u32[]{:S(2)}, u32[]{:S(2)}) collective-permute-start(f32[3,128,128]{2,1,0:T(8,128)} %surface.1), channel_id=1, source_target_pairs={{64,0},{65,1},{66,2},{67,3},{68,4},{69,5},{70,6},{71,7},{72,8},{73... | collective-permute-start | bytes 589832 | tf_op jit(solution)/shard_map/ppermute | solution.py:463
  47.6 19.8 %collective-permute-start.3 = (f32[128,128]{1,0:T(8,128)S(1)}, f32[128,128]{1,0:T(8,128)S(1)}, u32[]{:S(2)}, u32[]{:S(2)}) collective-permute-start(f32[128,128]{1,0:T(8,128)S(1)} %get-tuple-element.30), channel_id=1, source_target_pairs={{0,64},{1,65},{2,66},{3,67},{4,68},{5,69},{6,70},{7,71},{8,72},{9,... | collective-permute-start | bytes 196616 | tf_op jit(solution)/shard_map/ppermute | solution.py:505
  67.4 0.6 copy-start.2

commit v4 on v3

v4 whole, which is shorter than its diff:
```python
import functools

import jax
import jax.numpy as jnp
from jax import lax
from jax.experimental import pallas as pl
from jax.experimental.pallas import tpu as pltpu
from jax.sharding import PartitionSpec as P

HEAT_DIFFUSION = 0.12
VERTICAL_MIXING = 0.2
FLUX_GAIN = 0.5
CAPACITY = 16
CHUNK = CAPACITY + 2
UNROLL = 8
LEVELS = 8

f32, bf16, i32 = jnp.float32, jnp.bfloat16, jnp.int32
VMEM = pl.BlockSpec(memory_space=pltpu.VMEM)
SMEM = pl.BlockSpec(memory_space=pltpu.SMEM)
ANY = pl.BlockSpec(memory_space=pl.ANY)
HBM = pl.BlockSpec(memory_space=pltpu.HBM)


def iota(shape, axis):
    return lax.broadcasted_iota(i32, shape, axis)


def pack_kernel(
    tiles, sec, dest_in, block_in, row_in, state_in, depth_in, temp, merid,
    payload, slot_of, up, down, brief_up, brief_down, blank,
    dest, block, row, state, count, entry, edge, depth,
    nothing, index_sem, state_sem, edge_sem, blank_sem,
):
    levels = temp.shape[1]
    rows = temp.shape[2]
    blocks = dest.shape[0]
    pieces = state_sem.shape[0]
    piece = blocks // pieces

    @pl.when(sec[0] == 0)
    def _():
        indices = [
            pltpu.make_async_copy(source, target, index_sem.at[n])
            for n, (source, target) in enumerate(
                ((dest_in, dest), (block_in, block), (row_in, row))
            )
        ]
        states = [
            pltpu.make_async_copy(
                state_in.at[0, pl.ds(n * piece, piece)],
                state.at[pl.ds(n * piece, piece)],
                state_sem.at[n],
            )
            for n in range(pieces)
        ]
        for copy in indices + states:
            copy.start()
        nothing[...] = jnp.zeros_like(nothing)
        blanks = [
            pltpu.make_async_copy(
                nothing, blank.at[0, pl.ds(n * LEVELS, LEVELS)], blank_sem.at[n]
            )
            for n in range(levels // LEVELS)
        ]
        for copy in blanks:
            copy.start()

        for i in range(tiles):
            count[i] = 0
        entry[...] = jnp.full(entry.shape, -1.0, f32)
        is_block = (iota((1, 128), 1) & 32) == 0
        for copy in indices:
            copy.wait()

        def place(step, _):
            for j in range(UNROLL):
                i = step * UNROLL + j
                d = dest[i]
                c = count[d]
                count[d] = c + 1
                c = jnp.minimum(c, CAPACITY - 1)
                slot = d * CAPACITY + c
                slot_of[i] = slot
                payload[d * CHUNK + c] = state[i]
                entry[pl.ds(slot, 1), :] = jnp.where(is_block, block[i], row[i]).astype(f32)
            return 0

        for n in range(pieces):
            states[n].wait()
            lax.fori_loop(n * piece // UNROLL, (n + 1) * piece // UNROLL, place, 0)
        left = iota((8, 128), 1) < 64

        def entries_of(g, _):
            for j in range(8):
                d = g * 8 + j
                low = entry[pl.ds(pl.multiple_of(d * CAPACITY, 8), 8), :]
                high = entry[pl.ds(pl.multiple_of(d * CAPACITY + 8, 8), 8), :]
                both = jnp.where(left, low, high)
                payload[d * CHUNK + CAPACITY] = both[0:4]
                payload[d * CHUNK + CAPACITY + 1] = both[4:8]
            return 0

        lax.fori_loop(0, tiles // 8, entries_of, 0)
        for copy in blanks:
            copy.wait()

    @pl.when(sec[0] != 0)
    def _():
        depth_copy = pltpu.make_async_copy(depth_in.at[0], depth, index_sem.at[0])
        depth_copy.start()
        copies = [
            pltpu.make_async_copy(field.at[0, :, pl.ds(lo, 8), :], edge.at[n], edge_sem.at[n])
            for n, (field, lo) in enumerate(
                ((temp, rows - 8), (merid, rows - 8), (temp, 0), (merid, 0))
            )
        ]
        for copy in copies:
            copy.start()

        def none(step, _):
            for j in range(UNROLL):
                slot_of[step * UNROLL + j] = 0
            return 0

        lax.fori_loop(0, blocks // UNROLL, none, 0)
        depth_copy.wait()
        for side, line in ((up, rows - 1), (down, 0)):
            side[2 * levels :, :] = jnp.broadcast_to(
                depth[line : line + 1, :].astype(f32), (8, depth.shape[1])
            )
        for n, copy in enumerate(copies):
            copy.wait()
            side = up if n < 2 else down
            side[pl.ds((n % 2) * levels, levels), :] = edge[n, :, 7 if n < 2 else 0, :]
        for side, brief in ((up, brief_up), (down, brief_down)):
            for m in range(3):
                brief[m : m + 1, :] = side[m * levels : m * levels + 1, :]


def through(k, depth, t, t_next, speed, speed_next):
    return jnp.where(
        k < depth,
        HEAT_DIFFUSION * (t_next - t) - (0.25 * (speed + speed_next)) * (t + t_next),
        0.0,
    )


def inner_faces(k, t, u, v, depth_e, depth_n):
    rows, cells = t.shape
    first = iota((rows, cells), 0) == 0
    east = through(k, depth_e, t, pltpu.roll(t, cells - 1, 1), u, pltpu.roll(u, cells - 1, 1))
    north = through(k, depth_n, t, pltpu.roll(t, rows - 1, 0), v, pltpu.roll(v, rows - 1, 0))
    return (east - pltpu.roll(east, 1, 1)) + (
        north - jnp.where(first, 0.0, pltpu.roll(north, 1, 0))
    )


def inner_depths(d):
    rows, cells = d.shape
    last = iota((rows, cells), 0) == rows - 1
    return (
        jnp.minimum(d, pltpu.roll(d, cells - 1, 1)),
        jnp.where(last, 0, jnp.minimum(d, pltpu.roll(d, rows - 1, 0))),
    )


def bring(copies):
    for copy in copies:
        copy.start()
    for copy in copies:
        copy.wait()


def surface_kernel(
    sec, temp, zonal, merid, depth, south, north,
    top,
    t_in, u_in, v_in, d_in, edge, made, sem, out_sem,
):
    @pl.when(sec[0] != 0)
    def _():
        pairs = [
            (temp.at[0, 0:2], t_in),
            (zonal.at[0, 0], u_in),
            (merid.at[0, 0], v_in),
            (depth.at[0], d_in),
            (north, edge.at[0]),
            (south, edge.at[1]),
        ]
        bring([pltpu.make_async_copy(*pair, sem.at[n]) for n, pair in enumerate(pairs)])
        d = d_in[...]
        rows, cells = d.shape
        t, v = t_in[0], v_in[...]
        t_n, v_n, d_n = (edge[0, m : m + 1, :] for m in range(3))
        t_s, v_s, d_s = (edge[1, m : m + 1, :] for m in range(3))
        end = slice(rows - 1, rows)
        northmost = through(
            0, jnp.minimum(d[end], d_n.astype(i32)), t[end], t_n, v[end], v_n
        )
        southmost = through(0, jnp.minimum(d[0:1], d_s.astype(i32)), t_s, t[0:1], v_s, v[0:1])
        at = iota((rows, cells), 0)
        outer = jnp.where(at == rows - 1, northmost, 0.0) - jnp.where(at == 0, southmost, 0.0)
        below = jnp.where(1 < d, VERTICAL_MIXING * (t_in[1] - t), 0.0)
        base = t + (inner_faces(0, t, u_in[...], v, *inner_depths(d)) + outer) + below
        wet = jnp.where(d > 0, FLUX_GAIN, 0.0)
        patches = cells // 128
        for p in range(patches):
            part = slice(p * 128, p * 128 + 128)
            made[0, pl.ds(p, rows, stride=patches), :] = t[:, part]
            made[1, pl.ds(p, rows, stride=patches), :] = base[:, part]
            made[2, pl.ds(p, rows, stride=patches), :] = wet[:, part]
        bring([pltpu.make_async_copy(made, top, out_sem)])


def ocean_kernel(
    levels, temp, zonal, merid, depth_in,
    out,
    depth, depth_e, depth_n, carry, sem,
):
    rows, cells = depth.shape
    bring([pltpu.make_async_copy(depth_in.at[0], depth, sem)])
    e, n = inner_depths(depth[...])
    depth_e[...] = e
    depth_n[...] = n
    carry[...] = jnp.zeros_like(carry)

    def step(index, temp_in, beneath, zonal_in, merid_in, fresh):
        i = index.index[0]
        above = carry[...]
        for j in range(LEVELS):
            k = i * LEVELS + j
            t = temp_in[0, j]
            under = beneath[0, 0] if j == LEVELS - 1 else temp_in[0, j + 1]
            below = jnp.where(k + 1 < depth[...], VERTICAL_MIXING * (under - t), 0.0)
            inner = inner_faces(k, t, zonal_in[0, j], merid_in[0, j], depth_e[...], depth_n[...])
            fresh[0, j] = t + inner + (below - above)
            above = below
        carry[...] = above

    slab = pl.BlockSpec((1, LEVELS, rows, cells), lambda i: (0, i, 0, 0))
    next_level = pl.BlockSpec(
        (1, 1, rows, cells), lambda i: (0, jnp.minimum((i + 1) * LEVELS, levels - 1), 0, 0)
    )
    pltpu.emit_pipeline(
        step,
        grid=(levels // LEVELS,),
        in_specs=[slab, next_level, slab, slab],
        out_specs=[slab],
        _explicit_indices=True,
    )(temp, temp, zonal, merid, out)


def settle_kernel(
    levels, sec, up_in, down_in, south_in, north_in, fresh_in, middle, blank,
    out,
    up, down, south, north, fresh, field, northmost, southmost, side_sem, in_sem, out_sem,
):
    rows, cells = field.shape[1:]
    patches = cells // 128

    @pl.when(sec[0] != 0)
    def _():
        pairs = (
            (up_in, up), (down_in, down), (south_in, south), (north_in, north), (fresh_in, fresh)
        )
        sides = [pltpu.make_async_copy(*pair, side_sem.at[n]) for n, pair in enumerate(pairs)]
        parts = [pl.ds(n * LEVELS, LEVELS) for n in range(levels // LEVELS)]
        ins = [
            pltpu.make_async_copy(middle.at[0, part], field.at[part], in_sem.at[n])
            for n, part in enumerate(parts)
        ]
        outs = [
            pltpu.make_async_copy(field.at[part], out.at[0, part], out_sem.at[n])
            for n, part in enumerate(parts)
        ]
        for copy in sides + ins:
            copy.start()
        for copy in sides:
            copy.wait()
        own_n = up[2 * levels : 2 * levels + 1, :].astype(i32)
        own_s = down[2 * levels : 2 * levels + 1, :].astype(i32)
        d_n = jnp.minimum(own_n, north[2 * levels : 2 * levels + 1, :].astype(i32))
        d_s = jnp.minimum(own_s, south[2 * levels : 2 * levels + 1, :].astype(i32))
        for at in range(0, levels, 8):
            k = iota((8, cells), 0) + at
            t, v = slice(at, at + 8), slice(levels + at, levels + at + 8)
            northmost[t, :] = through(k, d_n, up[t, :], north[t, :], up[v, :], north[v, :])
            southmost[t, :] = through(k, d_s, south[t, :], down[t, :], south[v, :], down[v, :])
        for n in range(len(parts)):
            ins[n].wait()
            for k in range(n * LEVELS, (n + 1) * LEVELS):
                field[k, rows - 1 : rows, :] += northmost[k : k + 1, :]
                field[k, 0:1, :] -= southmost[k : k + 1, :]
            if n == 0:
                for p in range(patches):
                    field[0, :, p * 128 : p * 128 + 128] = fresh[pl.ds(p, rows, stride=patches), :]
            outs[n].start()
        for copy in outs:
            copy.wait()


def in_three(x):
    high = x.astype(bf16)
    rest = x - high.astype(f32)
    middle = rest.astype(bf16)
    low = (rest - middle.astype(f32)).astype(bf16)
    return jnp.concatenate([high, middle, low], axis=1)


def joined(x, at=0):
    return x[:, at : at + 128] + (x[:, at + 128 : at + 256] + x[:, at + 256 : at + 384])


def heat_kernel(tiles, sec, payload, top, table, ret, fresh, hit, weighted):
    slots = tiles * CAPACITY

    @pl.when(sec[0] != 0)
    def _():
        ret[...] = jnp.zeros_like(ret)
        fresh[...] = jnp.zeros_like(fresh)

    @pl.when(sec[0] == 0)
    def _():
        surface_parts = in_three(top[0])
        table_parts = in_three(
            jnp.concatenate([table[...], jnp.zeros((128 - table.shape[0], 128), f32)], axis=0)
        )
        lane = iota((1, 8, 128), 2).astype(f32)
        group = min(16, tiles)

        def step(g, _):
            base = pl.multiple_of(g * group, group)
            upper = payload[pl.ds(base * CHUNK, group * CHUNK)].reshape(group, CHUNK, 4, 128)
            entry = upper[:, CAPACITY:].reshape(group, 8, 128)
            at = pl.multiple_of(base * CAPACITY, group * CAPACITY)
            size = group * CAPACITY
            block_hit = jnp.concatenate(
                [entry[:, None, :, 0:1] == lane[None], entry[:, None, :, 64:65] == lane[None]],
                axis=1,
            ).reshape(size, 128)
            row_hit = jnp.concatenate(
                [entry[:, None, :, 32:33] == lane[None], entry[:, None, :, 96:97] == lane[None]],
                axis=1,
            ).reshape(size, 128)
            live = jnp.concatenate(
                [
                    jnp.broadcast_to(entry[:, None, :, 0:1], (group, 1, 8, 128)),
                    jnp.broadcast_to(entry[:, None, :, 64:65], (group, 1, 8, 128)),
                ],
                axis=1,
            ).reshape(size, 128) >= 0
            block_one = jnp.where(block_hit, 1.0, 0.0).astype(bf16)
            row_one = jnp.where(row_hit, 1.0, 0.0).astype(bf16)
            hit[pl.ds(at, size), :] = block_one
            surface = joined(jnp.dot(block_one, surface_parts, preferred_element_type=f32))
            weights = joined(jnp.dot(row_one, table_parts, preferred_element_type=f32))

            def channel(c):
                return upper[:, :CAPACITY, c, :].reshape(size, 128)

            contrast = surface - channel(1)
            transfer = 0.8 + 0.4 * jnp.tanh(contrast)
            saturation = 0.6 * jnp.exp(0.3 * surface)
            heat = channel(3) - transfer * channel(0) * (
                contrast + 1.5 * (saturation - channel(2))
            )
            product = jnp.where(live, weights * heat, 0.0)
            weighted[pl.ds(at, size), 0:384] = in_three(product)
            weighted[pl.ds(at, size), 384:768] = in_three(weights)
            return 0

        lax.fori_loop(0, tiles // group, step, 0)
        sums = lax.dot_general(
            hit[...], weighted[...], (((0,), (0,)), ((), ())), preferred_element_type=f32
        )
        forcing = joined(sums) / jnp.maximum(joined(sums, 384), 1.0)
        new_top = top[1] + top[2] * forcing
        fresh[...] = new_top
        ret[...] = joined(jnp.dot(hit[...], in_three(new_top), preferred_element_type=f32))


def nothing_kernel(*refs):
    pass


def body(
    atm_state, routes, dst_block, weight_index, area_table, ocean_temp, vel_u, vel_v, depth_levels
):
    tiles = lax.axis_size("tile")
    block_count = atm_state.shape[1]
    levels, rows, cells = ocean_temp.shape[1:]
    patches = rows * cells // 128
    slots = tiles * CAPACITY
    sec = lax.axis_index("sec").astype(i32).reshape(1)
    grant = pltpu.CompilerParams(vmem_limit_bytes=24 << 20)
    ocean_grant = pltpu.CompilerParams(vmem_limit_bytes=56 << 20)
    whole_grant = pltpu.CompilerParams(vmem_limit_bytes=60 << 20)

    edge_rows = 2 * levels + 8
    payload, slot_of, up, down, brief_up, brief_down, blank = pl.pallas_call(
        functools.partial(pack_kernel, tiles),
        out_shape=(
            jax.ShapeDtypeStruct((tiles * CHUNK, 4, 128), f32),
            jax.ShapeDtypeStruct((block_count,), i32),
            jax.ShapeDtypeStruct((edge_rows, cells), f32),
            jax.ShapeDtypeStruct((edge_rows, cells), f32),
            jax.ShapeDtypeStruct((8, cells), f32),
            jax.ShapeDtypeStruct((8, cells), f32),
            jax.ShapeDtypeStruct(ocean_temp.shape, f32),
        ),
        in_specs=[SMEM] + [HBM] * 7,
        out_specs=(VMEM, SMEM, VMEM, VMEM, VMEM, VMEM, HBM),
        scratch_shapes=[
            pltpu.SMEM((block_count,), i32),
            pltpu.SMEM((block_count,), i32),
            pltpu.SMEM((block_count,), i32),
            pltpu.VMEM((block_count, 4, 128), f32),
            pltpu.SMEM((tiles,), i32),
            pltpu.VMEM((slots, 128), f32),
            pltpu.VMEM((4, levels, 8, cells), f32),
            pltpu.VMEM((rows, cells), i32),
            pltpu.VMEM((LEVELS, rows, cells), f32),
            pltpu.SemaphoreType.DMA((3,)),
            pltpu.SemaphoreType.DMA((4,)),
            pltpu.SemaphoreType.DMA((4,)),
            pltpu.SemaphoreType.DMA((levels // LEVELS,)),
        ],
        compiler_params=whole_grant,
        name="pack",
    )(
        sec, routes.reshape(block_count), dst_block.reshape(block_count),
        weight_index.reshape(block_count), atm_state, depth_levels, ocean_temp, vel_v,
    )

    def unwritten(shapes):
        return pl.pallas_call(
            nothing_kernel,
            out_shape=shapes,
            out_specs=tuple(HBM for _ in shapes),
            compiler_params=ocean_grant,
            name="nothing",
        )()

    def from_sides(northmost, southmost):
        north_to = [(tiles + t, tiles + t + 1) for t in range(tiles - 1)]
        south_to = [(t + 1, t) for t in range(tiles, 2 * tiles - 1)]
        return (
            lax.ppermute(northmost, ("sec", "tile"), north_to),
            lax.ppermute(southmost, ("sec", "tile"), south_to),
        )

    top_shape = jax.ShapeDtypeStruct((3, patches, 128), f32)
    edge_shape = jax.ShapeDtypeStruct((edge_rows, cells), f32)
    field_shape = jax.ShapeDtypeStruct(ocean_temp.shape, f32)

    def split(atmosphere, ocean, *values):
        return lax.cond(sec[0] == 0, atmosphere, ocean, *values)

    def exchanged(value):
        return lax.all_to_all(value, "tile", split_axis=0, concat_axis=0, tiled=True)

    def surface(brief_up, brief_down):
        south, north = from_sides(brief_up, brief_down)
        return pl.pallas_call(
            surface_kernel,
            out_shape=top_shape,
            in_specs=[SMEM] + [HBM] * 4 + [ANY] * 2,
            out_specs=HBM,
            scratch_shapes=[
                pltpu.VMEM((2, rows, cells), f32),
                pltpu.VMEM((rows, cells), f32),
                pltpu.VMEM((rows, cells), f32),
                pltpu.VMEM((rows, cells), i32),
                pltpu.VMEM((2, 8, cells), f32),
                pltpu.VMEM((3, patches, 128), f32),
                pltpu.SemaphoreType.DMA((6,)),
                pltpu.SemaphoreType.DMA(()),
            ],
            compiler_params=ocean_grant,
            name="surface",
        )(sec, ocean_temp, vel_u, vel_v, depth_levels, south, north)

    def middle_of(temp, zonal, merid, depth):
        return pl.pallas_call(
            functools.partial(ocean_kernel, levels),
            in_specs=[HBM] * 4,
            out_specs=HBM,
            out_shape=field_shape,
            scratch_shapes=[
                pltpu.VMEM((rows, cells), i32),
                pltpu.VMEM((rows, cells), i32),
                pltpu.VMEM((rows, cells), i32),
                pltpu.VMEM((rows, cells), f32),
                pltpu.SemaphoreType.DMA(()),
            ],
            compiler_params=ocean_grant,
            name="ocean",
        )(temp, zonal, merid, depth)

    top = split(
        lambda up, down: unwritten((top_shape,))[0], surface, brief_up, brief_down
    )
    payload, up, down, top = lax.optimization_barrier((payload, up, down, top))
    top = lax.ppermute(top, "sec", [(1, 0)])

    def first_atmosphere(payload):
        payload, middle = lax.optimization_barrier((payload, unwritten((field_shape,))[0]))
        return exchanged(payload), middle

    moved, middle = split(
        first_atmosphere,
        lambda payload: (payload, middle_of(ocean_temp, vel_u, vel_v, depth_levels)),
        payload,
    )

    ret, fresh = pl.pallas_call(
        functools.partial(heat_kernel, tiles),
        out_shape=(
            jax.ShapeDtypeStruct((slots, 128), f32),
            jax.ShapeDtypeStruct((patches, 128), f32),
        ),
        in_specs=[SMEM, VMEM, VMEM, VMEM],
        out_specs=(VMEM, VMEM),
        scratch_shapes=[pltpu.VMEM((slots, 128), bf16), pltpu.VMEM((slots, 768), bf16)],
        compiler_params=grant,
        name="heat",
    )(sec, moved, top, area_table)
    fresh = lax.ppermute(fresh, "sec", [(0, 1)])

    def second_atmosphere(ret, up, down):
        ret, south, north = lax.optimization_barrier((ret, *unwritten((edge_shape, edge_shape))))
        return exchanged(ret), south, north

    back, south, north = split(
        second_atmosphere, lambda ret, up, down: (ret, *from_sides(up, down)), ret, up, down
    )
    skin = back.at[slot_of].get(mode="promise_in_bounds")
    following = pl.pallas_call(
        functools.partial(settle_kernel, levels),
        out_shape=field_shape,
        in_specs=[SMEM] + [ANY] * 5 + [HBM] * 2,
        out_specs=HBM,
        scratch_shapes=[pltpu.VMEM((edge_rows, cells), f32)] * 4
        + [
            pltpu.VMEM((patches, 128), f32),
            pltpu.VMEM((levels, rows, cells), f32),
            pltpu.VMEM((levels, cells), f32),
            pltpu.VMEM((levels, cells), f32),
            pltpu.SemaphoreType.DMA((5,)),
            pltpu.SemaphoreType.DMA((levels // LEVELS,)),
            pltpu.SemaphoreType.DMA((levels // LEVELS,)),
        ],
        input_output_aliases={7: 0},
        compiler_params=grant,
        name="settle",
    )(sec, up, down, south, north, fresh, middle, blank)
    return following, skin[None]


def solution(mesh):
    return jax.shard_map(
        body,
        mesh=mesh,
        in_specs=(
            P("sec", "tile", None, None),
            P("sec", "tile", None),
            P("sec", "tile"),
            P("sec", "tile"),
            P(),
            P("sec", None, "tile", None),
            P("sec", None, "tile", None),
            P("sec", None, "tile", None),
            P("sec", "tile", None),
        ),
        out_specs=(P("sec", None, "tile", None), P("sec", "tile", None)),
        check_vma=False,
    )
```

time: 69.4 us -> 65.3 us (0.941)
  the two profiles are of different devices: /device:TPU:0 before, /device:TPU:7 now
where the time goes in v4:
time: 65.3 us; the launch traced here: 64.8 us
  Pallas kernels  26.6 us (41%)
  starting transfers between devices  22.7 us (35%)
  waiting for transfers between devices  12.4 us (19%)
  local copies, waits for them, and re-layouts  2.27 us (3%)
  between operations  0.76 us (1%)
    ppermute x2, starting transfers between devices, from_sides(): lax.ppermute(southmost, ('sec', 'tile'), south_to)  14.6 us
    pallas_call x1, Pallas kernels, middle_of(): pl.pallas_call(functools.partial(ocean_kernel, levels), in_specs=[HBM] *...  14.4 us
    ppermute x2, waiting for transfers between devices, from_sides(): lax.ppermute(northmost, ('sec', 'tile'), north_to)  6.6 us
    ppermute x2, waiting for transfers between devices, from_sides(): lax.ppermute(southmost, ('sec', 'tile'), south_to)  5.8 us
    pallas_call x1, Pallas kernels, body(): pl.pallas_call(functools.partial(pack_kernel, tiles), out_shape=(jax.Shap...  5.56 us
    ppermute x2, starting transfers between devices, from_sides(): lax.ppermute(northmost, ('sec', 'tile'), north_to)  5.47 us
    pallas_call x1, Pallas kernels, body(): pl.pallas_call(functools.partial(settle_kernel, levels), out_shape=field_...  5.06 us
    gather x1, local copies, waits for them, and re-layouts, body(): skin = back.at[slot_of].get(mode='promise_in_bounds')  1.64 us
  transfers between devices with their start and end apart: 6, of which 3 were waited for; matrix products, arithmetic and copies ran while one was open for 3% of the time, Pallas kernels for 22%

profile of v4, /device:TPU:7, one launch (start us, length us, event | category | flops | bytes accessed | tf_op | source)
XLA Modules:
  0.0 64.8 jit_solution(9543614950838355457)
XLA Ops:
  0.6 0.0 copy-start.1
  0.6 5.6 %pack.1 = (f32[1152,4,128]{2,1,0:T(4,128)S(1)}, s32[512]{0:T(512)}, f32[168,1024]{1,0:T(8,128)}, f32[168,1024]{1,0:T(8,128)}, f32[8,1024]{1,0:T(8,128)S(1)}, /*i...) custom-call(s32[1]{0:T(128)} %bitcast.2.sec, s32[512]{0:T(512)} %bitcast.10, s32[512]{0:T(512)} %bitcast.11, s32[512]{0:T(512)} %bitcast.12, ...), custom_call_target="tpu_custom_call" | custom-call | tf_op jit(solution)/shard_map/pack/pallas_call | solution.py:400
  6.2 0.0 copy-done.1
  6.2 13.4 %conditional.3 = (f32[3,128,128]{2,1,0:T(8,128)S(1)}) conditional(s32[]{:T(128)} %convert_element_type.2, (f32[8,1024]{1,0:T(8,128)S(1)}, f32[8,1024]{1,0:T(8,128)S(1)}, s32[1]{0:T(128)}, f32[1,80,16,1024]{3,2,1,0:T(8,128)}, f32[1,80,16,1024]{3,2,1,0:T(8,128)}, /*index=5*/f32[1,80,16,1024]{3,2,1,0:T(8,128)}, s32[1,16,1024]{2,1,0:T(8,128)S(1)}) %tuple.45, ...), branch_computations={%region_0.0_spmd, %region_1.0_spmd} | conditional | bytes 524432 | solution.py:457
  6.2 3.5 %collective-permute-start = (f32[8,1024]{1,0:T(8,128)S(1)}, f32[8,1024]{1,0:T(8,128)S(1)}, u32[]{:S(2)}, u32[]{:S(2)}) collective-permute-start(f32[8,1024]{1,0:T(8,128)S(1)} %get-tuple-element.40), channel_id=1, source_target_pairs={{64,65},{65,66},{66,67},{67,68},{68,69},{69,70},{70,71},{71,72},{7... | collective-permute-start | bytes 98312 | tf_op jit(solution)/shard_map/cond/branch_0_fun/ppermute | solution.py:448
  9.8 6.8 %collective-permute-start.1 = (f32[8,1024]{1,0:T(8,128)S(1)}, f32[8,1024]{1,0:T(8,128)S(1)}, u32[]{:S(2)}, u32[]{:S(2)}) collective-permute-start(f32[8,1024]{1,0:T(8,128)S(1)} %get-tuple-element.41), channel_id=1, source_target_pairs={{65,64},{66,65},{67,66},{68,67},{69,68},{70,69},{71,70},{72,71},{7... | collective-permute-start | bytes 98312 | tf_op jit(solution)/shard_map/cond/branch_0_fun/ppermute | solution.py:449
  16.6 0.0 collective-permute-done.south
  16.6 0.0 copy-start.2
  16.6 1.0 %collective-permute-done.1.north = f32[8,1024]{1,0:T(8,128)S(1)} collective-permute-done((f32[8,1024]{1,0:T(8,128)S(1)}, f32[8,1024]{1,0:T(8,128)S(1)}, u32[]{:S(2)}, u32[]{:S(2)}) %collective-permute-start.1) | collective-permute-done | bytes 32800 | tf_op jit(solution)/shard_map/cond/branch_0_fun/ppermute | solution.py:449
  17.6 0.0 copy-start.3
  17.6 0.0 copy-done.2
  17.6 0.6 copy-done.3
  18.2 1.5 %surface.1 = f32[3,128,128]{2,1,0:T(8,128)S(1)} custom-call(s32[1]{0:T(128)} %get-tuple-element.35.sec, f32[1,80,16,1024]{3,2,1,0:T(8,128)} %get-tuple-element.36.temp, f32[1,80,16,1024]{3,2,1,0:T(8,128)} %get-tuple-element.37.zonal, f32[1,80,16,1024]{3,2,1,0:T(8,128)} %get-tuple-element.38.merid, s32[1,16,1024]{2,1,0:T(8,128)S(1)} %get-tuple-element.39.depth, ...), custom_call_target="tpu_custom_call" | custom-call | tf_op jit(solution)/shard_map/cond/branch_0_fun/surface/pallas_call | solution.py:464
  19.7 1.3 %collective-permute-start.4 = (f32[3,128,128]{2,1,0:T(8,128)S(1)}, f32[3,128,128]{2,1,0:T(8,128)S(1)}, u32[]{:S(2)}, u32[]{:S(2)}) collective-permute-start(f32[3,128,128]{2,1,0:T(8,128)S(1)} %get-tuple-element.105), channel_id=1, source_target_pairs={{64,0},{65,1},{66,2},{67,3},{68,4},{69,5},{70,6},{71,7},{72,8},{73... | collective-permute-start | bytes 589832 | tf_op jit(solution)/shard_map/ppermute | solution.py:504
  21.0 0.0 copy-start.4
  21.0 0.0 copy-start
  21.0 14.4 %conditional.4 = (f32[1152,4,128]{2,1,0:T(4,128)S(1)}, f32[1,80,16,1024]{3,2,1,0:T(8,128)}) conditional(s32[]{:T(128)} %convert_element_type.2, (f32[1,80,16,1024]{3,2,1,0:T(8,128)}, f32[1,80,16,1024]{3,2,1,0:T(8,128)}, f32[1,80,16,1024]{3,2,1,0:T(8,128)}, s32[1,16,1024]{2,1,0:T(8,128)S(1)}, f32[1152,4,128]{2,1,0:T(4,128)S(1)}) %tuple.46, ...), branch_computations={%region_2.0_spmd, %region_3.0_spmd} | conditional | bytes 9437200 | solution.py:457
  21.0 14.4 %ocean.1 = f32[1,80,16,1024]{3,2,1,0:T(8,128)} custom-call(f32[1,80,16,1024]{3,2,1,0:T(8,128)} %get-tuple-element.43.temp, f32[1,80,16,1024]{3,2,1,0:T(8,128)} %get-tuple-element.44.zonal, f32[1,80,16,1024]{3,2,1,0:T(8,128)} %get-tuple-element.45.merid, s32[1,16,1024]{2,1,0:T(8,128)S(1)} %get-tuple-element.46.depth_in), custom_call_target="tpu_custom_call" | custom-call | tf_op jit(solution)/shard_map/cond/branch_0_fun/ocean/pallas_call | solution.py:484
  35.5 0.0 copy-done.4
  35.5 0.0 collective-permute-done.4.top
  35.5 0.0 copy-done
  35.5 0.1 heat.1
  35.6 1.3 %collective-permute-start.5 = (f32[128,128]{1,0:T(8,128)S(1)}, f32[128,128]{1,0:T(8,128)S(1)}, u32[]{:S(2)}, u32[]{:S(2)}) collective-permute-start(f32[128,128]{1,0:T(8,128)S(1)} %get-tuple-element.90), channel_id=1, source_target_pairs={{0,64},{1,65},{2,66},{3,67},{4,68},{5,69},{6,70},{7,71},{8,72},{9,... | collective-permute-start | bytes 196616 | tf_op jit(solution)/shard_map/ppermute | solution.py:528
  36.9 21.2 %conditional.5 = (f32[1024,128]{1,0:T(8,128)S(1)}, f32[168,1024]{1,0:T(8,128)S(1)}, f32[168,1024]{1,0:T(8,128)S(1)}) conditional(s32[]{:T(128)} %convert_element_type.2, (f32[168,1024]{1,0:T(8,128)}, f32[168,1024]{1,0:T(8,128)}, f32[1024,128]{1,0:T(8,128)S(1)}) %tuple.37, f32[1024,128]{1,0:T(8,128)S(1)} %get-tuple-element.87), branch_computations={%region_4.0_spmd, %region_5.0_spmd} | conditional | bytes 5505128 | solution.py:457
  36.9 1.9 %collective-permute-start.2 = (f32[168,1024]{1,0:T(8,128)}, f32[168,1024]{1,0:T(8,128)S(1)}, u32[]{:S(2)}, u32[]{:S(2)}) collective-permute-start(f32[168,1024]{1,0:T(8,128)} %get-tuple-element.50), channel_id=1, source_target_pairs={{64,65},{65,66},{66,67},{67,68},{68,69},{69,70},{70,71},{71,72},{7... | collective-permute-start | bytes 2064392 | tf_op jit(solution)/shard_map/cond/branch_0_fun/ppermute | solution.py:448
  38.8 7.9 %collective-permute-start.3 = (f32[168,1024]{1,0:T(8,128)}, f32[168,1024]{1,0:T(8,128)S(1)}, u32[]{:S(2)}, u32[]{:S(2)}) collective-permute-start(f32[168,1024]{1,0:T(8,128)} %get-tuple-element.51), channel_id=1, source_target_pairs={{65,64},{66,65},{67,66},{68,67},{69,68},{70,69},{71,70},{72,71},{7... | collective-permute-start | bytes 2064392 | tf_op jit(solution)/shard_map/cond/branch_0_fun/ppermute | solution.py:449
  46.7 6.6 %collective-permute-done.2 = f32[168,1024]{1,0:T(8,128)S(1)} collective-permute-done((f32[168,1024]{1,0:T(8,128)}, f32[168,1024]{1,0:T(8,128)S(1)}, u32[]{:S(2)}, u32[]{:S(2)}) %collective-permute-start.2) | collective-permute-done | bytes 688160 | tf_op jit(solution)/shard_map/cond/branch_0_fun/ppermute | solution.py:448
  53.3 4.8 %collective-permute-done.3 = f32[168,1024]{1,0:T(8,128)S(1)} collective-permute-done((f32[168,1024]{1,0:T(8,128)}, f32[168,1024]{1,0:T(8,128)S(1)}, u32[]{:S(2)}, u32[]{:S(2)}) %collective-permute-start.3) | collective-permute-done | bytes 688160 | tf_op jit(solution)/shard_map/cond/branch_0_fun/ppermute | solution.py:449
  58.1 1.6 %gather_fusion = f32[512,128]{1,0:T(8,128)} fusion(f32[1024,128]{1,0:T(8,128)S(1)} %get-tuple-element.93, s32[1024]{0:T(1024)S(1)} %pad_clamp_fusion), kind=kCustom, calls=%fused_computation | custom fusion | bytes 526336 | tf_op jit(solution)/shard_map/gather | solution.py:537
  59.7 0.0 collective-permute-done.5.fresh_in
  59.8 5.1 %settle.1 = f32[1,80,16,1024]{3,2,1,0:T(8,128)} custom-call(s32[1]{0:T(128)} %bitcast.2.sec, f32[168,1024]{1,0:T(8,128)} %get-tuple-element.82.up_in, f32[168,1024]{1,0:T(8,128)} %get-tuple-element.83.down_in, f32[168,1024]{1,0:T(8,128)S(1)} %get-tuple-element.88.south_in, ...), custom_call_target="tpu_custom_call", output_to_operand_aliasing={{}: (7, {})} | custom-call | tf_op jit(solution)/shard_map/settle/pallas_call | solution.py:538
  (2 shorter events, 0.0 us)
Async XLA Ops:
  0.6 5.6 %copy-start.1 = (s32[1,16,1024]{2,1,0:T(8,128)S(1)}, s32[1,16,1024]{2,1,0:T(8,128)}, u32[]{:S(2)}) copy-start(s32[1,16,1024]{2,1,0:T(8,128)} %depth_in.1) | copy-start | bytes 196612
  6.2 10.3 %collective-permute-start = (f32[8,1024]{1,0:T(8,128)S(1)}, f32[8,1024]{1,0:T(8,128)S(1)}, u32[]{:S(2)}, u32[]{:S(2)}) collective-permute-start(f32[8,1024]{1,0:T(8,128)S(1)} %get-tuple-element.40), channel_id=1, source_target_pairs={{64,65},{65,66},{66,67},{67,68},{68,69},{69,70},{70,71},{71,72},{7... | collective-permute-start | bytes 98312 | tf_op jit(solution)/shard_map/cond/branch_0_fun/ppermute | solution.py:448
  9.8 7.8 %collective-permute-start.1 = (f32[8,1024]{1,0:T(8,128)S(1)}, f32[8,1024]{1,0:T(8,128)S(1)}, u32[]{:S(2)}, u32[]{:S(2)}) collective-permute-start(f32[8,1024]{1,0:T(8,128)S(1)} %get-tuple-element.41), channel_id=1, source_target_pairs={{65,64},{66,65},{67,66},{68,67},{69,68},{70,69},{71,70},{72,71},{7... | collective-permute-start | bytes 98312 | tf_op jit(solution)/shard_map/cond/branch_0_fun/ppermute | solution.py:449
  16.6 1.0 %copy-start.2 = (f32[8,1024]{1,0:T(8,128)}, f32[8,1024]{1,0:T(8,128)S(1)}, u32[]{:S(2)}) copy-start(f32[8,1024]{1,0:T(8,128)S(1)} %collective-permute-done.south) | copy-start | bytes 98308 | tf_op jit(solution)/shard_map/cond
  17.6 0.6 copy-start.3
  19.7 15.8 %collective-permute-start.4 = (f32[3,128,128]{2,1,0:T(8,128)S(1)}, f32[3,128,128]{2,1,0:T(8,128)S(1)}, u32[]{:S(2)}, u32[]{:S(2)}) collective-permute-start(f32[3,128,128]{2,1,0:T(8,128)S(1)} %get-tuple-element.105), channel_id=1, source_target_pairs={{64,0},{65,1},{66,2},{67,3},{68,4},{69,5},{70,6},{71,7},{72,8},{73... | collective-permute-start | bytes 589832 | tf_op jit(solution)/shard_map/ppermute | solution.py:504
  21.0 14.5 %copy-start.4 = (s32[512]{0:T(512)S(1)}, s32[512]{0:T(512)}, u32[]{:S(2)}) copy-start(s32[512]{0:T(512)} %get-tuple-element.94) | copy-start | bytes 6148
  21.0 14.5 %copy-start = (f32[16,128]{1,0:T(8,128)S(1)}, f32[16,128]{1,0:T(8,128)}, u32[]{:S(2)}) copy-start(f32[16,128]{1,0:T(8,128)} %table.1) | copy-start | bytes 24580
  35.6 24.2 %collective-permute-start.5 = (f32[128,128]{1,0:T(8,128)S(1)}, f32[128,128]{1,0:T(8,128)S(1)}, u32[]{:S(2)}, u32[]{:S(2)}) collective-permute-start(f32[128,128]{1,0:T(8,128)S(1)} %get-tuple-element.90), channel_id=1, source_target_pairs={{0,64},{1,65},{2,66},{3,67},{4,68},{5,69},{6,70},{7,71},{8,72},{9,... | collective-permute-start | bytes 196616 | tf_op jit(solution)/shard_map/ppermute | solution.py:528
  36.9 16.4 %collective-permute-start.2 = (f32[168,1024]{1,0:T(8,128)}, f32[168,1024]{1,0:T(8,128)S(1)}, u32[]{:S(2)}, u32[]{:S(2)}) collective-permute-start(f32[168,1024]{1,0:T(8,128)} %get-tuple-element.50), channel_id=1, source_target_pairs={{64,65},{65,66},{66,67},{67,68},{68,69},{69,70},{70,71},{71,72},{7... | collective-permute-start | bytes 2064392 | tf_op jit(solution)/shard_map/cond/branch_0_fun/ppermute | solution.py:448
  38.8 19.3 %collective-permute-start.3 = (f32[168,1024]{1,0:T(8,128)}, f32[168,1024]{1,0:T(8,128)S(1)}, u32[]{:S(2)}, u32[]{:S(2)}) collective-permute-start(f32[168,1024]{1,0:T(8,128)} %get-tuple-element.51), channel_id=1, source_target_pairs={{65,64},{66,65},{67,66},{68,67},{69,68},{70,69},{71,70},{72,71},{7... | collective-permute-start | bytes 2064392 | tf_op jit(solution)/shard_map/cond/branch_0_fun/ppermute | solution.py:449

commit v5 on v4

--- a/solution.py
+++ b/solution.py
@@ -13,7 +13,7 @@
 CAPACITY = 16
 CHUNK = CAPACITY + 2
 UNROLL = 8
-LEVELS = 8
+LEVELS = 16
 
 f32, bf16, i32 = jnp.float32, jnp.bfloat16, jnp.int32
 VMEM = pl.BlockSpec(memory_space=pltpu.VMEM)
@@ -67,8 +67,8 @@
             copy.start()
 
         for i in range(tiles):
-            count[i] = 0
-        entry[...] = jnp.full(entry.shape, -1.0, f32)
+            count[i] = i * CHUNK
+        entry[...] = jnp.full(entry.shape, -1, i32)
         is_block = (iota((1, 128), 1) & 32) == 0
         for copy in indices:
             copy.wait()
@@ -77,13 +77,11 @@
             for j in range(UNROLL):
                 i = step * UNROLL + j
                 d = dest[i]
-                c = count[d]
-                count[d] = c + 1
-                c = jnp.minimum(c, CAPACITY - 1)
-                slot = d * CAPACITY + c
-                slot_of[i] = slot
-                payload[d * CHUNK + c] = state[i]
-                entry[pl.ds(slot, 1), :] = jnp.where(is_block, block[i], row[i]).astype(f32)
+                place_of = count[d]
+                count[d] = place_of + 1
+                slot_of[i] = place_of
+                payload[place_of] = state[i]
+                entry[pl.ds(place_of, 1), :] = jnp.where(is_block, block[i], row[i])
             return 0
 
         for n in range(pieces):
@@ -94,9 +92,9 @@
         def entries_of(g, _):
             for j in range(8):
                 d = g * 8 + j
-                low = entry[pl.ds(pl.multiple_of(d * CAPACITY, 8), 8), :]
-                high = entry[pl.ds(pl.multiple_of(d * CAPACITY + 8, 8), 8), :]
-                both = jnp.where(left, low, high)
+                low = entry[pl.ds(d * CHUNK, 8), :]
+                high = entry[pl.ds(d * CHUNK + 8, 8), :]
+                both = jnp.where(left, low, high).astype(f32)
                 payload[d * CHUNK + CAPACITY] = both[0:4]
                 payload[d * CHUNK + CAPACITY + 1] = both[4:8]
             return 0
@@ -326,7 +324,7 @@
             jnp.concatenate([table[...], jnp.zeros((128 - table.shape[0], 128), f32)], axis=0)
         )
         lane = iota((1, 8, 128), 2).astype(f32)
-        group = min(16, tiles)
+        group = min(64, tiles)
 
         def step(g, _):
             base = pl.multiple_of(g * group, group)
@@ -416,7 +414,7 @@
             pltpu.SMEM((block_count,), i32),
             pltpu.VMEM((block_count, 4, 128), f32),
             pltpu.SMEM((tiles,), i32),
-            pltpu.VMEM((slots, 128), f32),
+            pltpu.VMEM((tiles * CHUNK, 128), i32),
             pltpu.VMEM((4, levels, 8, cells), f32),
             pltpu.VMEM((rows, cells), i32),
             pltpu.VMEM((LEVELS, rows, cells), f32),
@@ -534,7 +532,14 @@
     back, south, north = split(
         second_atmosphere, lambda ret, up, down: (ret, *from_sides(up, down)), ret, up, down
     )
-    skin = back.at[slot_of].get(mode="promise_in_bounds")
+    index = slot_of - (CHUNK - CAPACITY) * (slot_of // CHUNK)
+    whole_rows = lax.GatherDimensionNumbers(
+        offset_dims=(1,), collapsed_slice_dims=(0,), start_index_map=(0,)
+    )
+    skin = lax.gather(
+        back, index[:, None], whole_rows, (1, 128),
+        mode=lax.GatherScatterMode.PROMISE_IN_BOUNDS,
+    )
     following = pl.pallas_call(
         functools.partial(settle_kernel, levels),
         out_shape=field_shape,

time: 65.3 us -> 63.1 us (0.966)
  the two profiles are of different devices: /device:TPU:7 before, /device:TPU:0 now
where the time goes in v5:
time: 63.1 us; the launch traced here: 62.9 us
  blocking collectives  49.5 us (78%)
  Pallas kernels  8.07 us (13%)
  starting transfers between devices  2.59 us (4%)
  local copies, waits for them, and re-layouts  1.89 us (3%)
  between operations  0.73 us (1%)
    all_to_all x2, blocking collectives, exchanged(): lax.all_to_all(value, 'tile', split_axis=0, concat_axis=0, tiled=True)  49.5 us
    pallas_call x1, Pallas kernels, body(): pl.pallas_call(functools.partial(pack_kernel, tiles), out_shape=(jax.Shap...  4.94 us
    pallas_call x1, Pallas kernels, body(): pl.pallas_call(functools.partial(heat_kernel, tiles), out_shape=(jax.Shap...  2.99 us
    gather x1, local copies, waits for them, and re-layouts, body(): lax.gather(back, index[:, None], whole_rows, (1, 128), mode=lax.GatherSca...  1.64 us
    ppermute x1, starting transfers between devices, body(): fresh = lax.ppermute(fresh, 'sec', [(0, 1)])  1.29 us
    ppermute x1, starting transfers between devices, body(): top = lax.ppermute(top, 'sec', [(1, 0)])  1.29 us
  transfers between devices with their start and end apart: 2, of which 0 were waited for; matrix products, arithmetic and copies ran while one was open for 3% of the time, Pallas kernels for 0%

profile of v5, /device:TPU:0, one launch (start us, length us, event | category | flops | bytes accessed | tf_op | source)
XLA Modules:
  0.0 62.9 jit_solution(9046264825330846256)
XLA Ops:
  0.6 0.0 copy-start.1
  0.6 4.9 %pack.1 = (f32[1152,4,128]{2,1,0:T(4,128)S(1)}, s32[512]{0:T(512)}, f32[168,1024]{1,0:T(8,128)}, f32[168,1024]{1,0:T(8,128)}, f32[8,1024]{1,0:T(8,128)S(1)}, /*i...) custom-call(s32[1]{0:T(128)} %bitcast.2.sec, s32[512]{0:T(512)} %bitcast.10, s32[512]{0:T(512)} %bitcast.11, s32[512]{0:T(512)} %bitcast.12, ...), custom_call_target="tpu_custom_call" | custom-call | tf_op jit(solution)/shard_map/pack/pallas_call | solution.py:398
  5.6 0.0 copy-done.1
  5.6 1.3 %collective-permute-start.4 = (f32[3,128,128]{2,1,0:T(8,128)S(1)}, f32[3,128,128]{2,1,0:T(8,128)S(1)}, u32[]{:S(2)}, u32[]{:S(2)}) collective-permute-start(f32[3,128,128]{2,1,0:T(8,128)S(1)} %get-tuple-element.105), channel_id=1, source_target_pairs={{64,0},{65,1},{66,2},{67,3},{68,4},{69,5},{70,6},{71,7},{72,8},{73... | collective-permute-start | bytes 589832 | tf_op jit(solution)/shard_map/ppermute | solution.py:502
  6.9 0.0 copy-start.4
  7.0 0.0 copy-start
  7.0 33.2 %conditional.4 = (f32[1152,4,128]{2,1,0:T(4,128)S(1)}, f32[1,80,16,1024]{3,2,1,0:T(8,128)}) conditional(s32[]{:T(128)} %convert_element_type.2, (f32[1,80,16,1024]{3,2,1,0:T(8,128)}, f32[1,80,16,1024]{3,2,1,0:T(8,128)}, f32[1,80,16,1024]{3,2,1,0:T(8,128)}, s32[1,16,1024]{2,1,0:T(8,128)S(1)}, f32[1152,4,128]{2,1,0:T(4,128)S(1)}) %tuple.46, ...), branch_computations={%region_2.0_spmd, %region_3.0_spmd} | conditional | bytes 9437200 | solution.py:455
  7.0 0.2 copy.25
  7.2 33.0 %all_to_all.13 = f32[1152,4,128]{2,1,0:T(4,128)S(1)} all-to-all(f32[1152,4,128]{2,1,0:T(4,128)S(1)} %copy.25), channel_id=1, replica_groups=mesh['sec'=2,'tile'=64] {'tile'}, dimensions={0} | all-to-all | bytes 4718592 | tf_op jit(solution)/shard_map/cond/branch_1_fun/all_to_all | solution.py:458
  40.2 0.0 copy-done.4
  40.2 0.0 collective-permute-done.4.top
  40.2 0.0 copy-done
  40.2 3.0 %heat.1 = (f32[1024,128]{1,0:T(8,128)S(1)}, f32[128,128]{1,0:T(8,128)S(1)}) custom-call(s32[1]{0:T(128)} %bitcast.2.sec, f32[1152,4,128]{2,1,0:T(4,128)S(1)} %get-tuple-element.85.payload, f32[3,128,128]{2,1,0:T(8,128)S(1)} %collective-permute-done.4.top, f32[16,128]{1,0:T(8,128)S(1)} %copy-done), custom_call_target="tpu_custom_call" | custom-call | tf_op jit(solution)/shard_map/heat/pallas_call | solution.py:514
  43.2 1.3 %collective-permute-start.5 = (f32[128,128]{1,0:T(8,128)S(1)}, f32[128,128]{1,0:T(8,128)S(1)}, u32[]{:S(2)}, u32[]{:S(2)}) collective-permute-start(f32[128,128]{1,0:T(8,128)S(1)} %get-tuple-element.90), channel_id=1, source_target_pairs={{0,64},{1,65},{2,66},{3,67},{4,68},{5,69},{6,70},{7,71},{8,72},{9,... | collective-permute-start | bytes 196616 | tf_op jit(solution)/shard_map/ppermute | solution.py:526
  44.5 16.6 %conditional.5 = (f32[1024,128]{1,0:T(8,128)S(1)}, f32[168,1024]{1,0:T(8,128)S(1)}, f32[168,1024]{1,0:T(8,128)S(1)}) conditional(s32[]{:T(128)} %convert_element_type.2, (f32[168,1024]{1,0:T(8,128)}, f32[168,1024]{1,0:T(8,128)}, f32[1024,128]{1,0:T(8,128)S(1)}) %tuple.37, f32[1024,128]{1,0:T(8,128)S(1)} %get-tuple-element.87), branch_computations={%region_4.0_spmd, %region_5.0_spmd} | conditional | bytes 5505128 | solution.py:455
  44.6 16.5 %all_to_all.14 = f32[64,16,128]{2,1,0:T(8,128)S(1)} all-to-all(f32[64,16,128]{2,1,0:T(8,128)S(1)} %copy.26), channel_id=1, replica_groups=mesh['sec'=2,'tile'=64] {'tile'}, dimensions={0} | all-to-all | bytes 1048576 | tf_op jit(solution)/shard_map/cond/branch_1_fun/all_to_all | solution.py:458
  61.1 1.6 %gather_fusion = f32[512,128]{1,0:T(8,128)} fusion(f32[1024,128]{1,0:T(8,128)S(1)} %get-tuple-element.93, s32[1024]{0:T(1024)S(1)} %pad_clamp_fusion), kind=kCustom, calls=%fused_computation | custom fusion | bytes 526336 | tf_op jit(solution)/shard_map/gather | solution.py:539
  62.7 0.0 collective-permute-done.5.fresh_in
  62.7 0.1 settle.1
  (7 shorter events, 0.1 us)
Async XLA Ops:
  0.6 5.0 %copy-start.1 = (s32[1,16,1024]{2,1,0:T(8,128)S(1)}, s32[1,16,1024]{2,1,0:T(8,128)}, u32[]{:S(2)}) copy-start(s32[1,16,1024]{2,1,0:T(8,128)} %depth_in.1) | copy-start | bytes 196612
  5.6 34.5 %collective-permute-start.4 = (f32[3,128,128]{2,1,0:T(8,128)S(1)}, f32[3,128,128]{2,1,0:T(8,128)S(1)}, u32[]{:S(2)}, u32[]{:S(2)}) collective-permute-start(f32[3,128,128]{2,1,0:T(8,128)S(1)} %get-tuple-element.105), channel_id=1, source_target_pairs={{64,0},{65,1},{66,2},{67,3},{68,4},{69,5},{70,6},{71,7},{72,8},{73... | collective-permute-start | bytes 589832 | tf_op jit(solution)/shard_map/ppermute | solution.py:502
  6.9 33.2 %copy-start.4 = (s32[512]{0:T(512)S(1)}, s32[512]{0:T(512)}, u32[]{:S(2)}) copy-start(s32[512]{0:T(512)} %get-tuple-element.94) | copy-start | bytes 6148
  7.0 33.2 %copy-start = (f32[16,128]{1,0:T(8,128)S(1)}, f32[16,128]{1,0:T(8,128)}, u32[]{:S(2)}) copy-start(f32[16,128]{1,0:T(8,128)} %table.1) | copy-start | bytes 24580
  43.2 19.5 %collective-permute-start.5 = (f32[128,128]{1,0:T(8,128)S(1)}, f32[128,128]{1,0:T(8,128)S(1)}, u32[]{:S(2)}, u32[]{:S(2)}) collective-permute-start(f32[128,128]{1,0:T(8,128)S(1)} %get-tuple-element.90), channel_id=1, source_target_pairs={{0,64},{1,65},{2,66},{3,67},{4,68},{5,69},{6,70},{7,71},{8,72},{9,... | collective-permute-start | bytes 196616 | tf_op jit(solution)/shard_map/ppermute | solution.py:526

commit v6 on v5

--- a/solution.py
+++ b/solution.py
@@ -11,8 +11,8 @@
 VERTICAL_MIXING = 0.2
 FLUX_GAIN = 0.5
 CAPACITY = 16
-CHUNK = CAPACITY + 2
-UNROLL = 8
+CHUNK = CAPACITY + 1
+UNROLL = 16
 LEVELS = 16
 
 f32, bf16, i32 = jnp.float32, jnp.bfloat16, jnp.int32
@@ -69,7 +69,7 @@
         for i in range(tiles):
             count[i] = i * CHUNK
         entry[...] = jnp.full(entry.shape, -1, i32)
-        is_block = (iota((1, 128), 1) & 32) == 0
+        is_block = (iota((1, 128), 1) & 16) == 0
         for copy in indices:
             copy.wait()
 
@@ -87,16 +87,15 @@
         for n in range(pieces):
             states[n].wait()
             lax.fori_loop(n * piece // UNROLL, (n + 1) * piece // UNROLL, place, 0)
-        left = iota((8, 128), 1) < 64
+        quarter = iota((4, 128), 1) // 32
 
         def entries_of(g, _):
             for j in range(8):
                 d = g * 8 + j
-                low = entry[pl.ds(d * CHUNK, 8), :]
-                high = entry[pl.ds(d * CHUNK + 8, 8), :]
-                both = jnp.where(left, low, high).astype(f32)
-                payload[d * CHUNK + CAPACITY] = both[0:4]
-                payload[d * CHUNK + CAPACITY + 1] = both[4:8]
+                both = entry[pl.ds(d * CHUNK, 4), :]
+                for q in range(1, 4):
+                    both = jnp.where(quarter == q, entry[pl.ds(d * CHUNK + 4 * q, 4), :], both)
+                payload[d * CHUNK + CAPACITY] = both.astype(f32)
             return 0
 
         lax.fori_loop(0, tiles // 8, entries_of, 0)
@@ -323,32 +322,32 @@
         table_parts = in_three(
             jnp.concatenate([table[...], jnp.zeros((128 - table.shape[0], 128), f32)], axis=0)
         )
-        lane = iota((1, 8, 128), 2).astype(f32)
+        lane = iota((1, 4, 128), 2).astype(f32)
         group = min(64, tiles)
 
         def step(g, _):
             base = pl.multiple_of(g * group, group)
             upper = payload[pl.ds(base * CHUNK, group * CHUNK)].reshape(group, CHUNK, 4, 128)
-            entry = upper[:, CAPACITY:].reshape(group, 8, 128)
+            entry = upper[:, CAPACITY]
             at = pl.multiple_of(base * CAPACITY, group * CAPACITY)
             size = group * CAPACITY
-            block_hit = jnp.concatenate(
-                [entry[:, None, :, 0:1] == lane[None], entry[:, None, :, 64:65] == lane[None]],
-                axis=1,
-            ).reshape(size, 128)
-            row_hit = jnp.concatenate(
-                [entry[:, None, :, 32:33] == lane[None], entry[:, None, :, 96:97] == lane[None]],
-                axis=1,
-            ).reshape(size, 128)
-            live = jnp.concatenate(
-                [
-                    jnp.broadcast_to(entry[:, None, :, 0:1], (group, 1, 8, 128)),
-                    jnp.broadcast_to(entry[:, None, :, 64:65], (group, 1, 8, 128)),
-                ],
-                axis=1,
-            ).reshape(size, 128) >= 0
-            block_one = jnp.where(block_hit, 1.0, 0.0).astype(bf16)
-            row_one = jnp.where(row_hit, 1.0, 0.0).astype(bf16)
+
+            def named(offset):
+                return jnp.concatenate(
+                    [
+                        jnp.where(
+                            entry[:, None, :, 32 * q + offset : 32 * q + offset + 1] == lane[None],
+                            1.0, 0.0,
+                        )
+                        for q in range(4)
+                    ],
+                    axis=1,
+                ).reshape(size, 128)
+
+            block_hit = named(0)
+            block_one = block_hit.astype(bf16)
+            row_one = named(16).astype(bf16)
+            live = jnp.sum(block_hit, axis=1, keepdims=True) > 0
             hit[pl.ds(at, size), :] = block_one
             surface = joined(jnp.dot(block_one, surface_parts, preferred_element_type=f32))
             weights = joined(jnp.dot(row_one, table_parts, preferred_element_type=f32))
@@ -536,9 +535,13 @@
     whole_rows = lax.GatherDimensionNumbers(
         offset_dims=(1,), collapsed_slice_dims=(0,), start_index_map=(0,)
     )
-    skin = lax.gather(
-        back, index[:, None], whole_rows, (1, 128),
-        mode=lax.GatherScatterMode.PROMISE_IN_BOUNDS,
+    skin = split(
+        lambda back, index: lax.gather(
+            back, index[:, None], whole_rows, (1, 128),
+            mode=lax.GatherScatterMode.PROMISE_IN_BOUNDS,
+        ),
+        lambda back, index: back[:block_count],
+        back, index,
     )
     following = pl.pallas_call(
         functools.partial(settle_kernel, levels),

time: 63.1 us -> 62.3 us (0.987)
  transfers between devices with their start and end apart: 2 -> 2, of which waited for: 0 -> 0; matrix products, arithmetic and copies ran while one was open for 3% -> 2% of each run, Pallas kernels for 0% -> 0%
where the time goes in v6:
time: 62.3 us; the launch traced here: 62.1 us
  blocking collectives  48.9 us (78%)
  Pallas kernels  7.93 us (13%)
  starting transfers between devices  2.59 us (4%)
  local copies, waits for them, and re-layouts  1.81 us (3%)
  between operations  0.73 us (1%)
    all_to_all x2, blocking collectives, exchanged(): lax.all_to_all(value, 'tile', split_axis=0, concat_axis=0, tiled=True)  48.9 us
    pallas_call x1, Pallas kernels, body(): pl.pallas_call(functools.partial(pack_kernel, tiles), out_shape=(jax.Shap...  4.94 us
    pallas_call x1, Pallas kernels, body(): pl.pallas_call(functools.partial(heat_kernel, tiles), out_shape=(jax.Shap...  2.84 us
    ppermute x1, starting transfers between devices, body(): fresh = lax.ppermute(fresh, 'sec', [(0, 1)])  1.29 us
    ppermute x1, starting transfers between devices, body(): top = lax.ppermute(top, 'sec', [(1, 0)])  1.29 us
  transfers between devices with their start and end apart: 2, of which 0 were waited for; matrix products, arithmetic and copies ran while one was open for 2% of the time, Pallas kernels for 0%

profile of v6, /device:TPU:0, one launch (start us, length us, event | category | flops | bytes accessed | tf_op | source)
XLA Modules:
  0.0 62.1 jit_solution(12346342647674237742)
XLA Ops:
  0.6 0.0 copy-start.1
  0.6 4.9 %pack.1 = (f32[1088,4,128]{2,1,0:T(4,128)S(1)}, s32[512]{0:T(512)S(1)}, f32[168,1024]{1,0:T(8,128)}, f32[168,1024]{1,0:T(8,128)}, f32[8,1024]{1,0:T(8,128)S(1)},...) custom-call(s32[1]{0:T(128)} %bitcast.4.sec, s32[512]{0:T(512)} %bitcast.12, s32[512]{0:T(512)} %bitcast.13, ...), custom_call_target="tpu_custom_call" | custom-call | tf_op jit(solution)/shard_map/pack/pallas_call | solution.py:397
  5.6 0.0 copy-done.1
  5.6 1.3 %collective-permute-start.4 = (f32[3,128,128]{2,1,0:T(8,128)S(1)}, f32[3,128,128]{2,1,0:T(8,128)S(1)}, u32[]{:S(2)}, u32[]{:S(2)}) collective-permute-start(f32[3,128,128]{2,1,0:T(8,128)S(1)} %get-tuple-element.180), channel_id=1, source_target_pairs={{64,0},{65,1},{66,2},{67,3},{68,4},{69,5},{70,6},{71,7},{72,8},{73... | collective-permute-start | bytes 589832 | tf_op jit(solution)/shard_map/ppermute | solution.py:501
  6.9 0.0 copy-start
  6.9 32.5 %conditional.5 = (f32[1088,4,128]{2,1,0:T(4,128)S(1)}, f32[1,80,16,1024]{3,2,1,0:T(8,128)}) conditional(s32[]{:T(128)} %convert_element_type.2, (f32[1,80,16,1024]{3,2,1,0:T(8,128)}, f32[1,80,16,1024]{3,2,1,0:T(8,128)}, f32[1,80,16,1024]{3,2,1,0:T(8,128)}, s32[1,16,1024]{2,1,0:T(8,128)S(1)}, f32[1088,4,128]{2,1,0:T(4,128)S(1)}) %tuple.68, ...), branch_computations={%region_2.0_spmd, %region_3.0_spmd} | conditional | bytes 8912912 | solution.py:454
  7.0 0.2 copy.27
  7.2 32.3 %all_to_all.13 = f32[1088,4,128]{2,1,0:T(4,128)S(1)} all-to-all(f32[1088,4,128]{2,1,0:T(4,128)S(1)} %copy.27), channel_id=1, replica_groups=mesh['sec'=2,'tile'=64] {'tile'}, dimensions={0} | all-to-all | bytes 4456448 | tf_op jit(solution)/shard_map/cond/branch_1_fun/all_to_all | solution.py:457
  39.5 0.0 collective-permute-done.4.top
  39.5 0.0 copy-done
  39.5 2.8 %heat.1 = (f32[1024,128]{1,0:T(8,128)S(1)}, f32[128,128]{1,0:T(8,128)S(1)}) custom-call(s32[1]{0:T(128)} %bitcast.4.sec, f32[1088,4,128]{2,1,0:T(4,128)S(1)} %get-tuple-element.160.payload, f32[3,128,128]{2,1,0:T(8,128)S(1)} %collective-permute-done.4.top, f32[16,128]{1,0:T(8,128)S(1)} %copy-done), custom_call_target="tpu_custom_call" | custom-call | tf_op jit(solution)/shard_map/heat/pallas_call | solution.py:513
  42.3 1.3 %collective-permute-start.5 = (f32[128,128]{1,0:T(8,128)S(1)}, f32[128,128]{1,0:T(8,128)S(1)}, u32[]{:S(2)}, u32[]{:S(2)}) collective-permute-start(f32[128,128]{1,0:T(8,128)S(1)} %get-tuple-element.165), channel_id=1, source_target_pairs={{0,64},{1,65},{2,66},{3,67},{4,68},{5,69},{6,70},{7,71},{8,72},{9,... | collective-permute-start | bytes 196616 | tf_op jit(solution)/shard_map/ppermute | solution.py:525
  43.6 16.6 %conditional.6 = (f32[1024,128]{1,0:T(8,128)S(1)}, f32[168,1024]{1,0:T(8,128)S(1)}, f32[168,1024]{1,0:T(8,128)S(1)}) conditional(s32[]{:T(128)} %convert_element_type.2, (f32[168,1024]{1,0:T(8,128)}, f32[168,1024]{1,0:T(8,128)}, f32[1024,128]{1,0:T(8,128)S(1)}) %tuple.56, f32[1024,128]{1,0:T(8,128)S(1)} %get-tuple-element.162), branch_computations={%region_4.0_spmd, %region_5.0_spmd} | conditional | bytes 5505128 | solution.py:454
  43.7 16.6 %all_to_all.14 = f32[64,16,128]{2,1,0:T(8,128)S(1)} all-to-all(f32[64,16,128]{2,1,0:T(8,128)S(1)} %copy.28), channel_id=1, replica_groups=mesh['sec'=2,'tile'=64] {'tile'}, dimensions={0} | all-to-all | bytes 1048576 | tf_op jit(solution)/shard_map/cond/branch_1_fun/all_to_all | solution.py:457
  60.3 1.1 %conditional.7 = (f32[1,512,128]{2,1,0:T(8,128)S(1)}) conditional(s32[]{:T(128)} %convert_element_type.2, f32[1024,128]{1,0:T(8,128)S(1)} %get-tuple-element.168, (s32[512]{0:T(512)S(1)}, f32[1024,128]{1,0:T(8,128)S(1)}) %tuple.57), branch_computations={%region_6.7_spmd, %region_7.8_spmd} | conditional | flops 5632 | bytes 536584 | solution.py:454
  60.3 1.0 %gather_fusion = f32[512,128]{1,0:T(8,128)S(1)} fusion(f32[1024,128]{1,0:T(8,128)S(1)} %get-tuple-element.130, s32[1024]{0:T(1024)S(1)} %pad_clamp_fusion), kind=kCustom, calls=%fused_computation | custom fusion | bytes 526336 | tf_op jit(solution)/shard_map/cond/branch_1_fun/gather | solution.py:539
  61.3 0.0 copy-start.2
  61.4 0.0 collective-permute-done.5.fresh_in
  61.4 0.1 settle.1
  61.5 0.5 copy-done.2
  (7 shorter events, 0.1 us)
Async XLA Ops:
  0.6 5.0 %copy-start.1 = (s32[1,16,1024]{2,1,0:T(8,128)S(1)}, s32[1,16,1024]{2,1,0:T(8,128)}, u32[]{:S(2)}) copy-start(s32[1,16,1024]{2,1,0:T(8,128)} %depth_in.1) | copy-start | bytes 196612
  5.6 33.9 %collective-permute-start.4 = (f32[3,128,128]{2,1,0:T(8,128)S(1)}, f32[3,128,128]{2,1,0:T(8,128)S(1)}, u32[]{:S(2)}, u32[]{:S(2)}) collective-permute-start(f32[3,128,128]{2,1,0:T(8,128)S(1)} %get-tuple-element.180), channel_id=1, source_target_pairs={{64,0},{65,1},{66,2},{67,3},{68,4},{69,5},{70,6},{71,7},{72,8},{73... | collective-permute-start | bytes 589832 | tf_op jit(solution)/shard_map/ppermute | solution.py:501
  6.9 32.6 %copy-start = (f32[16,128]{1,0:T(8,128)S(1)}, f32[16,128]{1,0:T(8,128)}, u32[]{:S(2)}) copy-start(f32[16,128]{1,0:T(8,128)} %table.1) | copy-start | bytes 24580
  42.3 19.0 %collective-permute-start.5 = (f32[128,128]{1,0:T(8,128)S(1)}, f32[128,128]{1,0:T(8,128)S(1)}, u32[]{:S(2)}, u32[]{:S(2)}) collective-permute-start(f32[128,128]{1,0:T(8,128)S(1)} %get-tuple-element.165), channel_id=1, source_target_pairs={{0,64},{1,65},{2,66},{3,67},{4,68},{5,69},{6,70},{7,71},{8,72},{9,... | collective-permute-start | bytes 196616 | tf_op jit(solution)/shard_map/ppermute | solution.py:525
  61.3 0.7 %copy-start.2 = (f32[1,512,128]{2,1,0:T(8,128)}, f32[1,512,128]{2,1,0:T(8,128)S(1)}, u32[]{:S(2)}) copy-start(f32[1,512,128]{2,1,0:T(8,128)S(1)} %get-tuple-element.181) | copy-start | bytes 786436

commit v7 on v6

--- a/solution.py
+++ b/solution.py
@@ -418,7 +418,7 @@
             pltpu.VMEM((rows, cells), i32),
             pltpu.VMEM((LEVELS, rows, cells), f32),
             pltpu.SemaphoreType.DMA((3,)),
-            pltpu.SemaphoreType.DMA((4,)),
+            pltpu.SemaphoreType.DMA((8,)),
             pltpu.SemaphoreType.DMA((4,)),
             pltpu.SemaphoreType.DMA((levels // LEVELS,)),
         ],

time: 62.3 us -> 62.3 us (level)
  no operation moved by 1% of the time
where the time goes in v7:
time: 62.3 us; the launch traced here: 62 us
  blocking collectives  48.9 us (78%)
  Pallas kernels  7.88 us (13%)
  starting transfers between devices  2.59 us (4%)
  local copies, waits for them, and re-layouts  1.81 us (3%)
  between operations  0.73 us (1%)
    all_to_all x2, blocking collectives, exchanged(): lax.all_to_all(value, 'tile', split_axis=0, concat_axis=0, tiled=True)  48.9 us
    pallas_call x1, Pallas kernels, body(): pl.pallas_call(functools.partial(pack_kernel, tiles), out_shape=(jax.Shap...  4.88 us
    pallas_call x1, Pallas kernels, body(): pl.pallas_call(functools.partial(heat_kernel, tiles), out_shape=(jax.Shap...  2.84 us
    ppermute x1, starting transfers between devices, body(): fresh = lax.ppermute(fresh, 'sec', [(0, 1)])  1.29 us
    ppermute x1, starting transfers between devices, body(): top = lax.ppermute(top, 'sec', [(1, 0)])  1.29 us
  transfers between devices with their start and end apart: 2, of which 0 were waited for; matrix products, arithmetic and copies ran while one was open for 2% of the time, Pallas kernels for 0%

profile of v7, /device:TPU:0, one launch (start us, length us, event | category | flops | bytes accessed | tf_op | source)
XLA Modules:
  0.0 62.0 jit_solution(4586534190890304098)
XLA Ops:
  0.6 0.0 copy-start.1
  0.6 4.9 %pack.1 = (f32[1088,4,128]{2,1,0:T(4,128)S(1)}, s32[512]{0:T(512)S(1)}, f32[168,1024]{1,0:T(8,128)}, f32[168,1024]{1,0:T(8,128)}, f32[8,1024]{1,0:T(8,128)S(1)},...) custom-call(s32[1]{0:T(128)} %bitcast.4.sec, s32[512]{0:T(512)} %bitcast.12, s32[512]{0:T(512)} %bitcast.13, ...), custom_call_target="tpu_custom_call" | custom-call | tf_op jit(solution)/shard_map/pack/pallas_call | solution.py:397
  5.5 0.0 copy-done.1
  5.6 1.3 %collective-permute-start.4 = (f32[3,128,128]{2,1,0:T(8,128)S(1)}, f32[3,128,128]{2,1,0:T(8,128)S(1)}, u32[]{:S(2)}, u32[]{:S(2)}) collective-permute-start(f32[3,128,128]{2,1,0:T(8,128)S(1)} %get-tuple-element.180), channel_id=1, source_target_pairs={{64,0},{65,1},{66,2},{67,3},{68,4},{69,5},{70,6},{71,7},{72,8},{73... | collective-permute-start | bytes 589832 | tf_op jit(solution)/shard_map/ppermute | solution.py:501
  6.9 0.0 copy-start
  6.9 32.5 %conditional.5 = (f32[1088,4,128]{2,1,0:T(4,128)S(1)}, f32[1,80,16,1024]{3,2,1,0:T(8,128)}) conditional(s32[]{:T(128)} %convert_element_type.2, (f32[1,80,16,1024]{3,2,1,0:T(8,128)}, f32[1,80,16,1024]{3,2,1,0:T(8,128)}, f32[1,80,16,1024]{3,2,1,0:T(8,128)}, s32[1,16,1024]{2,1,0:T(8,128)S(1)}, f32[1088,4,128]{2,1,0:T(4,128)S(1)}) %tuple.68, ...), branch_computations={%region_2.0_spmd, %region_3.0_spmd} | conditional | bytes 8912912 | solution.py:454
  6.9 0.2 copy.27
  7.1 32.3 %all_to_all.13 = f32[1088,4,128]{2,1,0:T(4,128)S(1)} all-to-all(f32[1088,4,128]{2,1,0:T(4,128)S(1)} %copy.27), channel_id=1, replica_groups=mesh['sec'=2,'tile'=64] {'tile'}, dimensions={0} | all-to-all | bytes 4456448 | tf_op jit(solution)/shard_map/cond/branch_1_fun/all_to_all | solution.py:457
  39.4 0.0 collective-permute-done.4.top
  39.4 0.0 copy-done
  39.4 2.8 %heat.1 = (f32[1024,128]{1,0:T(8,128)S(1)}, f32[128,128]{1,0:T(8,128)S(1)}) custom-call(s32[1]{0:T(128)} %bitcast.4.sec, f32[1088,4,128]{2,1,0:T(4,128)S(1)} %get-tuple-element.160.payload, f32[3,128,128]{2,1,0:T(8,128)S(1)} %collective-permute-done.4.top, f32[16,128]{1,0:T(8,128)S(1)} %copy-done), custom_call_target="tpu_custom_call" | custom-call | tf_op jit(solution)/shard_map/heat/pallas_call | solution.py:513
  42.3 1.3 %collective-permute-start.5 = (f32[128,128]{1,0:T(8,128)S(1)}, f32[128,128]{1,0:T(8,128)S(1)}, u32[]{:S(2)}, u32[]{:S(2)}) collective-permute-start(f32[128,128]{1,0:T(8,128)S(1)} %get-tuple-element.165), channel_id=1, source_target_pairs={{0,64},{1,65},{2,66},{3,67},{4,68},{5,69},{6,70},{7,71},{8,72},{9,... | collective-permute-start | bytes 196616 | tf_op jit(solution)/shard_map/ppermute | solution.py:525
  43.6 16.6 %conditional.6 = (f32[1024,128]{1,0:T(8,128)S(1)}, f32[168,1024]{1,0:T(8,128)S(1)}, f32[168,1024]{1,0:T(8,128)S(1)}) conditional(s32[]{:T(128)} %convert_element_type.2, (f32[168,1024]{1,0:T(8,128)}, f32[168,1024]{1,0:T(8,128)}, f32[1024,128]{1,0:T(8,128)S(1)}) %tuple.56, f32[1024,128]{1,0:T(8,128)S(1)} %get-tuple-element.162), branch_computations={%region_4.0_spmd, %region_5.0_spmd} | conditional | bytes 5505128 | solution.py:454
  43.7 16.6 %all_to_all.14 = f32[64,16,128]{2,1,0:T(8,128)S(1)} all-to-all(f32[64,16,128]{2,1,0:T(8,128)S(1)} %copy.28), channel_id=1, replica_groups=mesh['sec'=2,'tile'=64] {'tile'}, dimensions={0} | all-to-all | bytes 1048576 | tf_op jit(solution)/shard_map/cond/branch_1_fun/all_to_all | solution.py:457
  60.2 1.1 %conditional.7 = (f32[1,512,128]{2,1,0:T(8,128)S(1)}) conditional(s32[]{:T(128)} %convert_element_type.2, f32[1024,128]{1,0:T(8,128)S(1)} %get-tuple-element.168, (s32[512]{0:T(512)S(1)}, f32[1024,128]{1,0:T(8,128)S(1)}) %tuple.57), branch_computations={%region_6.7_spmd, %region_7.8_spmd} | conditional | flops 5632 | bytes 536584 | solution.py:454
  60.3 1.0 %gather_fusion = f32[512,128]{1,0:T(8,128)S(1)} fusion(f32[1024,128]{1,0:T(8,128)S(1)} %get-tuple-element.130, s32[1024]{0:T(1024)S(1)} %pad_clamp_fusion), kind=kCustom, calls=%fused_computation | custom fusion | bytes 526336 | tf_op jit(solution)/shard_map/cond/branch_1_fun/gather | solution.py:539
  61.3 0.0 copy-start.2
  61.3 0.0 collective-permute-done.5.fresh_in
  61.3 0.1 settle.1
  61.5 0.5 copy-done.2
  (7 shorter events, 0.1 us)
Async XLA Ops:
  0.6 4.9 %copy-start.1 = (s32[1,16,1024]{2,1,0:T(8,128)S(1)}, s32[1,16,1024]{2,1,0:T(8,128)}, u32[]{:S(2)}) copy-start(s32[1,16,1024]{2,1,0:T(8,128)} %depth_in.1) | copy-start | bytes 196612
  5.6 33.9 %collective-permute-start.4 = (f32[3,128,128]{2,1,0:T(8,128)S(1)}, f32[3,128,128]{2,1,0:T(8,128)S(1)}, u32[]{:S(2)}, u32[]{:S(2)}) collective-permute-start(f32[3,128,128]{2,1,0:T(8,128)S(1)} %get-tuple-element.180), channel_id=1, source_target_pairs={{64,0},{65,1},{66,2},{67,3},{68,4},{69,5},{70,6},{71,7},{72,8},{73... | collective-permute-start | bytes 589832 | tf_op jit(solution)/shard_map/ppermute | solution.py:501
  6.9 32.6 %copy-start = (f32[16,128]{1,0:T(8,128)S(1)}, f32[16,128]{1,0:T(8,128)}, u32[]{:S(2)}) copy-start(f32[16,128]{1,0:T(8,128)} %table.1) | copy-start | bytes 24580
  42.3 19.0 %collective-permute-start.5 = (f32[128,128]{1,0:T(8,128)S(1)}, f32[128,128]{1,0:T(8,128)S(1)}, u32[]{:S(2)}, u32[]{:S(2)}) collective-permute-start(f32[128,128]{1,0:T(8,128)S(1)} %get-tuple-element.165), channel_id=1, source_target_pairs={{0,64},{1,65},{2,66},{3,67},{4,68},{5,69},{6,70},{7,71},{8,72},{9,... | collective-permute-start | bytes 196616 | tf_op jit(solution)/shard_map/ppermute | solution.py:525
  61.3 0.7 %copy-start.2 = (f32[1,512,128]{2,1,0:T(8,128)}, f32[1,512,128]{2,1,0:T(8,128)S(1)}, u32[]{:S(2)}) copy-start(f32[1,512,128]{2,1,0:T(8,128)S(1)} %get-tuple-element.181) | copy-start | bytes 786436
